TPU v7x, 128 devices: a whole 4x4x4 slice. The times are simulated.
128 devices in a mesh: row: 16 (over y_lo, x, core), col: 8 (over y_hi, z).
Axes of the slice: x: 4, y: 4 (y_hi: 2, y_lo: 2; y = y_hi * 2 + y_lo), z: 4, core: 2. Of those that a mesh axis runs over, the one named last changes fastest.
Arguments:
- features: bfloat16 [32768, 256], P(('row', 'col')), may hold values from -6 to 6
- adjacency: bfloat16 [128, 384, 128, 128], P(('row', 'col')), may hold values from -0.046875 to 0.046875
- tile_row: int32 [128, 384], P(('row', 'col')), may hold values from 0 to 15, as said below
- tile_column: int32 [128, 384], P(('row', 'col')), may hold values from 0 to 31, as said below
- tile_count: int32 [128], P(('row', 'col')), may hold values from 1 to 384, as said below
- weight_in: bfloat16 [256, 1024], replicated, may hold values from -0.375 to 0.375
- bias_in: float32 [1024], replicated, may hold values from -3 to 3
- weight_out: bfloat16 [1024, 256], replicated, may hold values from -0.25 to 0.25
- bias_out: float32 [256], replicated, may hold values from -3 to 3
Outputs:
- updated: bfloat16 [32768, 256], P(('row', 'col'))
Inputs may be any that keep to these rules, and one draw needn't show every extreme that they name: `tile_row`: for every device and slot s < tile_count, the block row i and block column j of step one satisfy i >= j, and no device names one pair twice. Slots at or beyond tile_count hold coordinates in range that are not part of A. Every device of the highest index along row holds exactly 384 tiles. `tile_column`: see tile_row. `tile_count`: every device of the highest index along row has the most.
All inputs are finite; a program needn't handle non-finite values.
Results may differ from a plain program's by a relative error of at most 0.0056.
Values may be sent and summed in bfloat16 or wider, within the bound.
No kernel may reach another device: no remote copies, remote signals or barrier semaphores. Data moves between devices by JAX's collectives and lax.ppermute only.
A program may use at most 128 MiB of HBM per device.

v0:
```python
import functools

import jax
import jax.numpy as jnp
from jax import lax
from jax.experimental import pallas as pl
from jax.experimental.pallas import tpu as pltpu
from jax.sharding import PartitionSpec as P


T = 128
BLK = 256
ROWS = 16
COLS = 32
CAP = 384
CHUNKS = 12
CT = CAP // CHUNKS
UNROLL = 16
HOPS = (0, 1, 3, 2)
BF = jnp.bfloat16
F32 = jnp.float32
MIB = 2**20
VMEM = pl.BlockSpec(memory_space=pltpu.VMEM)
HBM = pl.BlockSpec(memory_space=pltpu.HBM)
SDS = jax.ShapeDtypeStruct


def row_perm(value, move):
    pairs = []
    for y in range(2):
        for x in range(4):
            for e in range(2):
                ty, tx, te = move(y, x, e)
                pairs.append(((y * 4 + x) * 2 + e, (ty * 4 + tx) * 2 + te))
    return lax.ppermute(value, "row", pairs)


def col_perm(value, move):
    pairs = []
    for y in range(2):
        for z in range(4):
            ty, tz = move(y, z)
            pairs.append((y * 4 + z, ty * 4 + tz))
    return lax.ppermute(value, "col", pairs)


def to_x(value, d):
    return row_perm(value, lambda y, x, e: (y, (x + d) % 4, e))


def to_ylo(value):
    return row_perm(value, lambda y, x, e: (1 - y, x, e))


def to_core(value):
    return row_perm(value, lambda y, x, e: (y, x, 1 - e))


def to_z(value, d):
    return col_perm(value, lambda y, z: (y, (z + d) % 4))


def to_yhi(value):
    return col_perm(value, lambda y, z: (1 - y, z))


def dense_kernel(places, tiles, panel_out, panel_t, held, panel, place_s, sems, place_sem, out_sem):
    place_copy = pltpu.make_async_copy(places, place_s, place_sem)
    place_copy.start()

    def fetch(q):
        part = pl.ds(q * CT, CT)
        return pltpu.make_async_copy(tiles.at[part], held.at[part], sems.at[q])

    for q in range(CHUNKS):
        fetch(q).start()

    def clear(j, _):
        panel[j] = jnp.zeros((ROWS * T, T), BF)
        return 0

    def clear_t(i, _):
        panel_t[i] = jnp.zeros((COLS * T, T), BF)
        return 0

    lax.fori_loop(0, COLS, clear, 0)
    place_copy.wait()
    count = place_s[0, CAP]

    def spot(s):
        at = place_s[0, s]
        return lax.div(at, COLS), lax.rem(at, COLS)

    def put(s):
        i, j = spot(s)
        panel[j, pl.ds(pl.multiple_of(i * T, T), T), :] = held[s]

    def put_t(s):
        i, j = spot(s)
        panel_t[i, pl.ds(pl.multiple_of(j * T, T), T), :] = held[s].T

    def each(low, live, step):
        def many(g, _):
            for u in range(UNROLL):
                step(low + g * UNROLL + u)
            return 0

        def one(s, _):
            step(s)
            return 0

        groups = lax.div(live, UNROLL)
        lax.fori_loop(0, groups, many, 0)
        lax.fori_loop(low + groups * UNROLL, low + live, one, 0)

    for q in range(CHUNKS):
        fetch(q).wait()
        each(q * CT, jnp.clip(count - q * CT, 0, CT), put)
    out_copy = pltpu.make_async_copy(panel, panel_out, out_sem)
    out_copy.start()
    lax.fori_loop(0, ROWS, clear_t, 0)
    each(0, count, put_t)
    out_copy.wait()


def slots(tile_row, tile_column, tile_count):
    spots = jnp.pad(tile_row * COLS + tile_column, ((0, 0), (0, T)))
    at = lax.broadcasted_iota(jnp.int32, spots.shape, 1)
    return jnp.where(at == CAP, tile_count[0], spots)


def dense(tiles, places):
    return pl.pallas_call(
        dense_kernel,
        out_shape=(
            SDS((COLS, ROWS * T, T), BF),
            pltpu.VMEM((ROWS, COLS * T, T), BF),
        ),
        in_specs=[HBM, HBM],
        out_specs=(HBM, VMEM),
        scratch_shapes=[
            pltpu.VMEM((CAP, T, T), BF),
            pltpu.VMEM((COLS, ROWS * T, T), BF),
            pltpu.SMEM((1, CAP + T), jnp.int32),
            pltpu.SemaphoreType.DMA((CHUNKS,)),
            pltpu.SemaphoreType.DMA,
            pltpu.SemaphoreType.DMA,
        ],
        compiler_params=pltpu.CompilerParams(vmem_limit_bytes=30 * MIB),
        cost_estimate=pl.CostEstimate(flops=0, bytes_accessed=45 * MIB, transcendentals=0),
        name="dense",
    )(places, tiles)


def row_place():
    r = lax.axis_index("row")
    return lax.div(r, 8), lax.rem(lax.div(r, 2), 4), lax.rem(r, 2)


def col_place():
    c = lax.axis_index("col")
    return lax.div(c, 4), lax.rem(c, 4)


def row_of(place, hop, flip, swap):
    y, x, e = place
    y = 1 - y if flip else y
    e = 1 - e if swap else e
    return (y * 4 + lax.rem(x + hop, 4)) * 2 + e


def col_of(place, hop, flip):
    y, z = place
    y = 1 - y if flip else y
    return y * 4 + lax.rem(z + hop, 4)


def block_rows(k):
    return pl.ds(pl.multiple_of(k * BLK, BLK), BLK)


def back_kernel(panel_t, *refs, targets):
    sources = refs[:4]
    outs = refs[4:]
    here, there = col_place(), row_place()
    rhs = jnp.concatenate([ref[...] for ref in sources], axis=0)
    order = []
    for hop in HOPS:
        for flip in range(2):
            c = col_of(here, (4 - hop) % 4, flip)
            order += [2 * c, 2 * c + 1]
    for n, (hop, swap) in enumerate(targets):
        lhs = []
        for flip in range(2):
            k = row_of(there, hop, flip, swap)
            part = block_rows(k)
            lhs.append(jnp.concatenate([panel_t[i, part, :] for i in order], axis=1))
        lhs = jnp.concatenate(lhs, axis=0)
        product = jnp.dot(lhs, rhs, preferred_element_type=F32)
        if len(outs) == 1:
            outs[0][n * 2 * BLK : (n + 1) * 2 * BLK, :] = product.astype(BF)
        else:
            outs[n][...] = product.astype(BF)


def back(panel_t, sources, targets, joined):
    n = len(targets)
    if joined:
        out_shape, out_specs = (SDS((n * 2 * BLK, BLK), BF),), (VMEM,)
    else:
        out_shape, out_specs = (SDS((2 * BLK, BLK), BF),) * n, (VMEM,) * n
    return pl.pallas_call(
        functools.partial(back_kernel, targets=targets),
        out_shape=out_shape,
        in_specs=[VMEM] * 5,
        out_specs=out_specs,
        compiler_params=pltpu.CompilerParams(vmem_limit_bytes=8 * MIB),
        cost_estimate=pl.CostEstimate(
            flops=2 * n * 512 * 2048 * 256, bytes_accessed=n * MIB, transcendentals=0
        ),
        name="back",
    )(panel_t, *sources)


def forward_kernel(panel, *refs, targets):
    sources = refs[:8]
    outs = refs[8:]
    here, there = col_place(), row_place()
    rhs = jnp.concatenate([ref[...] for ref in sources], axis=0)
    order = []
    for swap in range(2):
        for hop in HOPS:
            for flip in range(2):
                k = row_of(there, (4 - hop) % 4, flip, swap)
                order += [2 * k, 2 * k + 1]
    for (hop, flip), out in zip(targets, outs):
        part = block_rows(col_of(here, hop, flip))
        lhs = jnp.concatenate([panel[j, part, :] for j in order], axis=1)
        out[...] = jnp.dot(lhs, rhs, preferred_element_type=F32).astype(out.dtype)


def forward(panel, sources, targets, dtype=BF):
    n = len(targets)
    return pl.pallas_call(
        functools.partial(forward_kernel, targets=targets),
        out_shape=(SDS((BLK, BLK), dtype),) * n,
        in_specs=[VMEM] * 9,
        out_specs=(VMEM,) * n,
        compiler_params=pltpu.CompilerParams(vmem_limit_bytes=8 * MIB),
        cost_estimate=pl.CostEstimate(
            flops=2 * n * 256 * 4096 * 256, bytes_accessed=n * MIB // 2, transcendentals=0
        ),
        name="forward",
    )(panel, *sources)


def join_kernel(recv, *refs):
    own, outs = refs[:4], refs[4:]
    for n in range(4):
        part = recv[n * 2 * BLK : (n + 1) * 2 * BLK, :].astype(F32)
        outs[n][...] = (own[n][...].astype(F32) + part).astype(BF)


def join(recv, own):
    return pl.pallas_call(
        join_kernel,
        out_shape=(SDS((2 * BLK, BLK), BF),) * 4,
        in_specs=[VMEM] * 5,
        out_specs=(VMEM,) * 4,
        compiler_params=pltpu.CompilerParams(vmem_limit_bytes=4 * MIB),
        name="join",
    )(recv, *own)


def pair_kernel(x, high, low, row_pair, col_pair):
    row_pair[:BLK] = x[...]
    row_pair[BLK:] = high[...]
    col_pair[:BLK] = x[...]
    col_pair[BLK:] = low[...]


def pair(x, high, low):
    return pl.pallas_call(
        pair_kernel,
        out_shape=(SDS((2 * BLK, BLK), BF),) * 2,
        in_specs=[VMEM] * 3,
        out_specs=(VMEM,) * 2,
        compiler_params=pltpu.CompilerParams(vmem_limit_bytes=4 * MIB),
        name="pair",
    )(x, high, low)


def stage_kernel(x, out, sem):
    copy = pltpu.make_async_copy(x, out, sem)
    copy.start()
    copy.wait()


def stage(x):
    return pl.pallas_call(
        stage_kernel,
        out_shape=pltpu.VMEM(x.shape, x.dtype),
        in_specs=[HBM],
        out_specs=VMEM,
        scratch_shapes=[pltpu.SemaphoreType.DMA],
        compiler_params=pltpu.CompilerParams(vmem_limit_bytes=4 * MIB),
        name="stage",
    )(x)


def total_kernel(*refs):
    total = refs[0][...].astype(F32)
    for ref in refs[1:-1]:
        total = total + ref[...].astype(F32)
    refs[-1][...] = total.astype(BF)


def total(*parts):
    return pl.pallas_call(
        total_kernel,
        out_shape=SDS(parts[0].shape, BF),
        in_specs=[VMEM] * len(parts),
        out_specs=VMEM,
        compiler_params=pltpu.CompilerParams(vmem_limit_bytes=4 * MIB),
        name="total",
    )(*parts)


def fold_kernel(own, a, b, c, keep, send):
    total = own[...].astype(F32) + a[...].astype(F32) + b[...].astype(F32) + c[...].astype(F32)
    keep[...] = total[:BLK]
    send[...] = total[BLK:].astype(BF)


def fold(own, arrived):
    return pl.pallas_call(
        fold_kernel,
        out_shape=(SDS((BLK, BLK), F32), SDS((BLK, BLK), BF)),
        in_specs=[VMEM] * 4,
        out_specs=(VMEM, VMEM),
        compiler_params=pltpu.CompilerParams(vmem_limit_bytes=4 * MIB),
        name="fold",
    )(own, *arrived)


def update_kernel(*refs):
    x, parts = refs[0], refs[1:-5]
    w_in, b_in, w_out, b_out, out = refs[-5:]
    total = parts[0][...].astype(F32)
    for ref in parts[1:]:
        total = total + ref[...].astype(F32)
    combined = (x[...].astype(F32) + total).astype(BF)
    hidden = jnp.dot(combined, w_in[...], preferred_element_type=F32) + b_in[...]
    hidden = jnp.maximum(hidden, 0.0).astype(BF)
    updated = jnp.dot(hidden, w_out[...], preferred_element_type=F32) + b_out[...]
    out[...] = updated.astype(BF)


def update(x, parts, w_in, b_in, w_out, b_out):
    return pl.pallas_call(
        update_kernel,
        out_shape=SDS((BLK, BLK), BF),
        in_specs=[VMEM] * (len(parts) + 5),
        out_specs=VMEM,
        compiler_params=pltpu.CompilerParams(vmem_limit_bytes=6 * MIB),
        name="update",
    )(x, *parts, w_in, b_in.reshape(1, -1), w_out, b_out.reshape(1, -1))


def shards(
    features, adjacency, tile_row, tile_column, tile_count, weight_in, bias_in, weight_out, bias_out
):
    high, low = to_yhi(features), to_ylo(features)
    own_features = stage(features)
    places = slots(tile_row, tile_column, tile_count)
    own_features, places = lax.optimization_barrier((own_features, places))
    row_pair, col_pair = pair(own_features, high, low)
    row_pairs, col_pairs = [row_pair], [col_pair]
    for d in HOPS[1:]:
        col_pairs.append(to_x(col_pair, d))
        row_pairs.append(to_z(row_pair, d))

    places, _ = lax.optimization_barrier((places, (row_pair, col_pair)))
    panel, panel_t = dense(adjacency[0], places)
    col_pairs = col_pairs + [to_core(block) for block in col_pairs]

    (to_other,) = back(panel_t, row_pairs, tuple((h, 1) for h in HOPS), True)
    from_other = to_core(to_other)
    own = back(panel_t, row_pairs, tuple((h, 0) for h in HOPS), False)
    chip = join(from_other, own)
    arrived = [to_x(chip[n], HOPS[n]) for n in (1, 2, 3)]

    sent = [forward(panel, col_pairs, tuple((h, flip) for h in HOPS[1:])) for flip in (1, 0)]
    on, here = ([to_z(block, h) for block, h in zip(part, HOPS[1:])] for part in sent)
    stay, turn = forward(panel, col_pairs, ((0, 0), (0, 1)), F32)

    col_keep, col_send = fold(chip[0], arrived)
    col_recv = to_ylo(col_send)
    row_recv = to_yhi(total(turn, *on))
    return update(
        own_features,
        (stay, *here, row_recv, col_keep, col_recv),
        weight_in,
        bias_in,
        weight_out,
        bias_out,
    )


def solution(mesh):
    placed = (
        P(("row", "col"), None),
        P(("row", "col"), None, None, None),
        P(("row", "col"), None),
        P(("row", "col"), None),
        P(("row", "col")),
        P(),
        P(),
        P(),
        P(),
    )
    return jax.shard_map(
        shards, mesh=mesh, in_specs=placed, out_specs=P(("row", "col"), None), check_vma=False
    )
```

profile of v0, /device:TPU:48, one launch (start us, length us, event | category | flops | bytes accessed | tf_op | source)
XLA Modules:
  0.0 79.4 jit_solution(15553586410253317820)
XLA Ops:
  0.3 2.2 %collective-permute-start.1 = (bf16[256,256]{1,0:T(8,128)(2,1)}, bf16[256,256]{1,0:T(8,128)(2,1)S(1)}, u32[]{:S(2)}, u32[]{:S(2)}) collective-permute-start(bf16[256,256]{1,0:T(8,128)(2,1)} %x.3), channel_id=1, source_target_pairs={{0,64},{8,72},{16,80},{24,88},{32,96},{40,104},{48,112},{56,120},{... | collective-permute-start | bytes 393224 | tf_op jit(solution)/shard_map/ppermute | solution.py:35
  2.5 0.7 multiply_add_fusion
  3.2 0.9 %copy-done.3 = bf16[256,256]{1,0:T(8,128)(2,1)S(1)} copy-done((bf16[256,256]{1,0:T(8,128)(2,1)S(1)}, bf16[256,256]{1,0:T(8,128)(2,1)}, u32[]{:S(2)}) %copy-start.3) | copy-done | bytes 131096
  4.9 3.1 %collective-permute-done.high = bf16[256,256]{1,0:T(8,128)(2,1)S(1)} collective-permute-done((bf16[256,256]{1,0:T(8,128)(2,1)}, bf16[256,256]{1,0:T(8,128)(2,1)S(1)}, u32[]{:S(2)}, u32[]{:S(2)}) %collective-permute-start) | collective-permute-done | bytes 131104 | tf_op jit(solution)/shard_map/ppermute | solution.py:44
  8.8 2.0 %collective-permute-start.16 = (bf16[512,256]{1,0:T(8,128)(2,1)S(1)}, bf16[512,256]{1,0:T(8,128)(2,1)S(1)}, u32[]{:S(2)}, u32[]{:S(2)}) collective-permute-start(bf16[512,256]{1,0:T(8,128)(2,1)S(1)} %get-tuple-element.32.refs_0_), channel_id=1, source_target_pairs={{0,1},{1,2},{2,3},{3,0},{4,5},{5,6},{6,7},{7,4},{8,9},{9,10},{10,1... | collective-permute-start | bytes 786440 | tf_op jit(solution)/shard_map/ppermute | solution.py:44
  10.9 3.0 %collective-permute-start.18 = (bf16[512,256]{1,0:T(8,128)(2,1)S(1)}, bf16[512,256]{1,0:T(8,128)(2,1)S(1)}, u32[]{:S(2)}, u32[]{:S(2)}) collective-permute-start(bf16[512,256]{1,0:T(8,128)(2,1)S(1)} %get-tuple-element.32.refs_0_), channel_id=1, source_target_pairs={{0,2},{1,3},{2,0},{3,1},{4,6},{5,7},{6,4},{7,5},{8,10},{9,11},{10,... | collective-permute-start | bytes 786440 | tf_op jit(solution)/shard_map/ppermute | solution.py:44
  13.9 10.5 %dense.1 = (bf16[32,2048,128]{2,1,0:T(8,128)(2,1)}, bf16[16,4096,128]{2,1,0:T(8,128)(2,1)S(1)}) custom-call(s32[1,512]{1,0:T(1,128)S(1)} %compare_select_fusion.places, bf16[384,128,128]{2,1,0:T(8,128)(2,1)} %bitcast.7), custom_call_target="tpu_custom_call" | custom-call | bytes 47185920 | tf_op jit(solution)/shard_map/dense/pallas_call | solution.py:133
  24.4 2.3 %back.2 = bf16[2048,256]{1,0:T(8,128)(2,1)S(1)} custom-call(bf16[16,4096,128]{2,1,0:T(8,128)(2,1)S(1)} %get-tuple-element.44.panel_t, bf16[512,256]{1,0:T(8,128)(2,1)S(1)} %get-tuple-element.32.refs_0_, bf16[512,256]{1,0:T(8,128)(2,1)S(1)} %collective-permute-done.16.refs_1_, bf16[512,256]{1,0:T(8,128)(2,1)S(1)} %collective-permute-done.17.refs_2_, ...), custom_call_target="tpu_custom_call" | custom-call | flops 2147483648 | bytes 4194304 | tf_op jit(solution)/shard_map/back/pallas_call | solution.py:212
  26.8 1.6 %collective-permute-start.2 = (bf16[512,256]{1,0:T(8,128)(2,1)S(1)}, bf16[512,256]{1,0:T(8,128)(2,1)S(1)}, u32[]{:S(2)}, u32[]{:S(2)}) collective-permute-start(bf16[512,256]{1,0:T(8,128)(2,1)S(1)} %get-tuple-element.33.refs_0_), channel_id=1, source_target_pairs={{0,16},{8,24},{16,32},{24,40},{32,48},{40,56},{48,0},{56,8},{64,80... | collective-permute-start | bytes 786440 | tf_op jit(solution)/shard_map/ppermute | solution.py:35
  28.4 1.7 %collective-permute-start.3 = (bf16[512,256]{1,0:T(8,128)(2,1)S(1)}, bf16[512,256]{1,0:T(8,128)(2,1)S(1)}, u32[]{:S(2)}, u32[]{:S(2)}) collective-permute-start(bf16[512,256]{1,0:T(8,128)(2,1)S(1)} %get-tuple-element.33.refs_0_), channel_id=1, source_target_pairs={{0,48},{8,56},{16,0},{24,8},{32,16},{40,24},{48,32},{56,40},{64,11... | collective-permute-start | bytes 786440 | tf_op jit(solution)/shard_map/ppermute | solution.py:35
  30.1 1.8 %collective-permute-start.4 = (bf16[512,256]{1,0:T(8,128)(2,1)S(1)}, bf16[512,256]{1,0:T(8,128)(2,1)S(1)}, u32[]{:S(2)}, u32[]{:S(2)}) collective-permute-start(bf16[512,256]{1,0:T(8,128)(2,1)S(1)} %get-tuple-element.33.refs_0_), channel_id=1, source_target_pairs={{0,32},{8,40},{16,48},{24,56},{32,0},{40,8},{48,16},{56,24},{64,96... | collective-permute-start | bytes 786440 | tf_op jit(solution)/shard_map/ppermute | solution.py:35
  31.9 4.8 %collective-permute-done.2.refs_1_ = bf16[512,256]{1,0:T(8,128)(2,1)S(1)} collective-permute-done((bf16[512,256]{1,0:T(8,128)(2,1)S(1)}, bf16[512,256]{1,0:T(8,128)(2,1)S(1)}, u32[]{:S(2)}, u32[]{:S(2)}) %collective-permute-start.2) | collective-permute-done | bytes 262176 | tf_op jit(solution)/shard_map/ppermute | solution.py:35
  36.7 4.9 %collective-permute-done.3.refs_2_ = bf16[512,256]{1,0:T(8,128)(2,1)S(1)} collective-permute-done((bf16[512,256]{1,0:T(8,128)(2,1)S(1)}, bf16[512,256]{1,0:T(8,128)(2,1)S(1)}, u32[]{:S(2)}, u32[]{:S(2)}) %collective-permute-start.3) | collective-permute-done | bytes 262176 | tf_op jit(solution)/shard_map/ppermute | solution.py:35
  41.7 1.7 %collective-permute-done.4.refs_3_ = bf16[512,256]{1,0:T(8,128)(2,1)S(1)} collective-permute-done((bf16[512,256]{1,0:T(8,128)(2,1)S(1)}, bf16[512,256]{1,0:T(8,128)(2,1)S(1)}, u32[]{:S(2)}, u32[]{:S(2)}) %collective-permute-start.4) | collective-permute-done | bytes 262176 | tf_op jit(solution)/shard_map/ppermute | solution.py:35
  43.4 1.5 %collective-permute-done.8.refs_7_ = bf16[512,256]{1,0:T(8,128)(2,1)S(1)} collective-permute-done((bf16[512,256]{1,0:T(8,128)(2,1)S(1)}, bf16[512,256]{1,0:T(8,128)(2,1)S(1)}, u32[]{:S(2)}, u32[]{:S(2)}) %collective-permute-start.8) | collective-permute-done | bytes 262176 | tf_op jit(solution)/shard_map/ppermute | solution.py:35
  44.9 1.8 %forward.5 = (bf16[256,256]{1,0:T(8,128)(2,1)S(1)}, bf16[256,256]{1,0:T(8,128)(2,1)S(1)}, bf16[256,256]{1,0:T(8,128)(2,1)S(1)}) custom-call(bf16[32,2048,128]{2,1,0:T(8,128)(2,1)S(1)} %copy-done, bf16[512,256]{1,0:T(8,128)(2,1)S(1)} %get-tuple-element.33.refs_0_, bf16[512,256]{1,0:T(8,128)(2,1)S(1)} %collective-permute-done.2.refs_1_, ...), custom_call_target="tpu_custom_call" | custom-call | flops 1610612736 | bytes 1572864 | tf_op jit(solution)/shard_map/forward/pallas_call | solution.py:244
  46.7 0.8 collective-permute-start.12
  47.4 2.3 %back.3 = (bf16[512,256]{1,0:T(8,128)(2,1)S(1)}, bf16[512,256]{1,0:T(8,128)(2,1)S(1)}, bf16[512,256]{1,0:T(8,128)(2,1)S(1)}, bf16[512,256]{1,0:T(8,128)(2,1)S(1)}) custom-call(bf16[16,4096,128]{2,1,0:T(8,128)(2,1)S(1)} %get-tuple-element.44.panel_t, bf16[512,256]{1,0:T(8,128)(2,1)S(1)} %get-tuple-element.32.refs_0_, ...), custom_call_target="tpu_custom_call" | custom-call | flops 2147483648 | bytes 4194304 | tf_op jit(solution)/shard_map/back/pallas_call | solution.py:212
  50.0 1.2 %collective-permute-start.20 = (bf16[512,256]{1,0:T(8,128)(2,1)S(1)}, bf16[512,256]{1,0:T(8,128)(2,1)S(1)}, u32[]{:S(2)}, u32[]{:S(2)}) collective-permute-start(bf16[512,256]{1,0:T(8,128)(2,1)S(1)} %get-tuple-element.50), channel_id=1, source_target_pairs={{0,16},{8,24},{16,32},{24,40},{32,48},{40,56},{48,0},{56,8},{64,80... | collective-permute-start | bytes 786440 | tf_op jit(solution)/shard_map/ppermute | solution.py:35
  51.2 2.1 %collective-permute-start.21 = (bf16[512,256]{1,0:T(8,128)(2,1)S(1)}, bf16[512,256]{1,0:T(8,128)(2,1)S(1)}, u32[]{:S(2)}, u32[]{:S(2)}) collective-permute-start(bf16[512,256]{1,0:T(8,128)(2,1)S(1)} %get-tuple-element.51), channel_id=1, source_target_pairs={{0,48},{8,56},{16,0},{24,8},{32,16},{40,24},{48,32},{56,40},{64,11... | collective-permute-start | bytes 786440 | tf_op jit(solution)/shard_map/ppermute | solution.py:35
  53.9 1.4 %collective-permute-start.13 = (bf16[256,256]{1,0:T(8,128)(2,1)S(1)}, bf16[256,256]{1,0:T(8,128)(2,1)S(1)}, u32[]{:S(2)}, u32[]{:S(2)}) collective-permute-start(bf16[256,256]{1,0:T(8,128)(2,1)S(1)} %get-tuple-element.42), channel_id=1, source_target_pairs={{0,3},{1,0},{2,1},{3,2},{4,7},{5,4},{6,5},{7,6},{8,11},{9,8},{10,9... | collective-permute-start | bytes 393224 | tf_op jit(solution)/shard_map/ppermute | solution.py:44
  55.3 1.2 %forward.3 = (f32[256,256]{1,0:T(8,128)S(1)}, f32[256,256]{1,0:T(8,128)S(1)}) custom-call(bf16[32,2048,128]{2,1,0:T(8,128)(2,1)S(1)} %copy-done, bf16[512,256]{1,0:T(8,128)(2,1)S(1)} %get-tuple-element.33.refs_0_, bf16[512,256]{1,0:T(8,128)(2,1)S(1)} %collective-permute-done.2.refs_1_, bf16[512,256]{1,0:T(8,128)(2,1)S(1)} %collective-permute-done.3.refs_2_, ...), custom_call_target="tpu_custom_call" | custom-call | flops 1073741824 | bytes 1048576 | tf_op jit(solution)/shard_map/forward/pallas_call | solution.py:244
  56.6 1.6 %collective-permute-start.14 = (bf16[256,256]{1,0:T(8,128)(2,1)S(1)}, bf16[256,256]{1,0:T(8,128)(2,1)S(1)}, u32[]{:S(2)}, u32[]{:S(2)}) collective-permute-start(bf16[256,256]{1,0:T(8,128)(2,1)S(1)} %get-tuple-element.43), channel_id=1, source_target_pairs={{0,2},{1,3},{2,0},{3,1},{4,6},{5,7},{6,4},{7,5},{8,10},{9,11},{10,... | collective-permute-start | bytes 393224 | tf_op jit(solution)/shard_map/ppermute | solution.py:44
  58.2 1.8 %forward.4 = (bf16[256,256]{1,0:T(8,128)(2,1)S(1)}, bf16[256,256]{1,0:T(8,128)(2,1)S(1)}, bf16[256,256]{1,0:T(8,128)(2,1)S(1)}) custom-call(bf16[32,2048,128]{2,1,0:T(8,128)(2,1)S(1)} %copy-done, bf16[512,256]{1,0:T(8,128)(2,1)S(1)} %get-tuple-element.33.refs_0_, bf16[512,256]{1,0:T(8,128)(2,1)S(1)} %collective-permute-done.2.refs_1_, ...), custom_call_target="tpu_custom_call" | custom-call | flops 1610612736 | bytes 1572864 | tf_op jit(solution)/shard_map/forward/pallas_call | solution.py:244
  60.0 3.0 %collective-permute-start.10 = (bf16[256,256]{1,0:T(8,128)(2,1)S(1)}, bf16[256,256]{1,0:T(8,128)(2,1)S(1)}, u32[]{:S(2)}, u32[]{:S(2)}) collective-permute-start(bf16[256,256]{1,0:T(8,128)(2,1)S(1)} %get-tuple-element.38), channel_id=1, source_target_pairs={{0,3},{1,0},{2,1},{3,2},{4,7},{5,4},{6,5},{7,6},{8,11},{9,8},{10,9... | collective-permute-start | bytes 393224 | tf_op jit(solution)/shard_map/ppermute | solution.py:44
  63.3 2.4 %collective-permute-start.11 = (bf16[256,256]{1,0:T(8,128)(2,1)S(1)}, bf16[256,256]{1,0:T(8,128)(2,1)S(1)}, u32[]{:S(2)}, u32[]{:S(2)}) collective-permute-start(bf16[256,256]{1,0:T(8,128)(2,1)S(1)} %get-tuple-element.39), channel_id=1, source_target_pairs={{0,2},{1,3},{2,0},{3,1},{4,6},{5,7},{6,4},{7,5},{8,10},{9,11},{10,... | collective-permute-start | bytes 393224 | tf_op jit(solution)/shard_map/ppermute | solution.py:44
  65.8 2.7 %collective-permute-start.9 = (bf16[256,256]{1,0:T(8,128)(2,1)S(1)}, bf16[256,256]{1,0:T(8,128)(2,1)S(1)}, u32[]{:S(2)}, u32[]{:S(2)}) collective-permute-start(bf16[256,256]{1,0:T(8,128)(2,1)S(1)} %get-tuple-element.37), channel_id=1, source_target_pairs={{0,1},{1,2},{2,3},{3,0},{4,5},{5,6},{6,7},{7,4},{8,9},{9,10},{10,1... | collective-permute-start | bytes 393224 | tf_op jit(solution)/shard_map/ppermute | solution.py:44
  68.5 1.7 %collective-permute-start.15 = (bf16[256,256]{1,0:T(8,128)(2,1)S(1)}, bf16[256,256]{1,0:T(8,128)(2,1)S(1)}, u32[]{:S(2)}, u32[]{:S(2)}) collective-permute-start(bf16[256,256]{1,0:T(8,128)(2,1)S(1)} %total.1), channel_id=1, source_target_pairs={{0,4},{1,5},{2,6},{3,7},{4,0},{5,1},{6,2},{7,3},{8,12},{9,13},{10,... | collective-permute-start | bytes 393224 | tf_op jit(solution)/shard_map/ppermute | solution.py:44
  70.3 3.7 %collective-permute-start.23 = (bf16[256,256]{1,0:T(8,128)(2,1)S(1)}, bf16[256,256]{1,0:T(8,128)(2,1)S(1)}, u32[]{:S(2)}, u32[]{:S(2)}) collective-permute-start(bf16[256,256]{1,0:T(8,128)(2,1)S(1)} %get-tuple-element.54), channel_id=1, source_target_pairs={{0,64},{8,72},{16,80},{24,88},{32,96},{40,104},{48,112},{56,120},{... | collective-permute-start | bytes 393224 | tf_op jit(solution)/shard_map/ppermute | solution.py:35
  74.0 0.9 %collective-permute-done.15.refs_5_ = bf16[256,256]{1,0:T(8,128)(2,1)S(1)} collective-permute-done((bf16[256,256]{1,0:T(8,128)(2,1)S(1)}, bf16[256,256]{1,0:T(8,128)(2,1)S(1)}, u32[]{:S(2)}, u32[]{:S(2)}) %collective-permute-start.15) | collective-permute-done | bytes 131104 | tf_op jit(solution)/shard_map/ppermute | solution.py:44
  74.9 3.2 %collective-permute-done.23.refs_7_ = bf16[256,256]{1,0:T(8,128)(2,1)S(1)} collective-permute-done((bf16[256,256]{1,0:T(8,128)(2,1)S(1)}, bf16[256,256]{1,0:T(8,128)(2,1)S(1)}, u32[]{:S(2)}, u32[]{:S(2)}) %collective-permute-start.23) | collective-permute-done | bytes 131104 | tf_op jit(solution)/shard_map/ppermute | solution.py:35
  78.1 1.2 %update.1 = bf16[256,256]{1,0:T(8,128)(2,1)} custom-call(bf16[256,256]{1,0:T(8,128)(2,1)S(1)} %stage.1.x.refs_0_, f32[256,256]{1,0:T(8,128)S(1)} %get-tuple-element.36.refs_1_, bf16[256,256]{1,0:T(8,128)(2,1)S(1)} %collective-permute-done.9.refs_2_, bf16[256,256]{1,0:T(8,128)(2,1)S(1)} %collective-permute-done.10.refs_3_, ...), custom_call_target="tpu_custom_call" | custom-call | tf_op jit(solution)/shard_map/update/pallas_call | solution.py:360
  (42 shorter events, 2.7 us)
Async XLA Ops:
  0.0 8.1 %collective-permute-start = (bf16[256,256]{1,0:T(8,128)(2,1)}, bf16[256,256]{1,0:T(8,128)(2,1)S(1)}, u32[]{:S(2)}, u32[]{:S(2)}) collective-permute-start(bf16[256,256]{1,0:T(8,128)(2,1)} %x.3), channel_id=1, source_target_pairs={{0,4},{1,5},{2,6},{3,7},{4,0},{5,1},{6,2},{7,3},{8,12},{9,13},{10,... | collective-permute-start | bytes 393224 | tf_op jit(solution)/shard_map/ppermute | solution.py:44
  0.3 8.4 %collective-permute-start.1 = (bf16[256,256]{1,0:T(8,128)(2,1)}, bf16[256,256]{1,0:T(8,128)(2,1)S(1)}, u32[]{:S(2)}, u32[]{:S(2)}) collective-permute-start(bf16[256,256]{1,0:T(8,128)(2,1)} %x.3), channel_id=1, source_target_pairs={{0,64},{8,72},{16,80},{24,88},{32,96},{40,104},{48,112},{56,120},{... | collective-permute-start | bytes 393224 | tf_op jit(solution)/shard_map/ppermute | solution.py:35
  3.2 0.9 %copy-start.3 = (bf16[256,256]{1,0:T(8,128)(2,1)S(1)}, bf16[256,256]{1,0:T(8,128)(2,1)}, u32[]{:S(2)}) copy-start(bf16[256,256]{1,0:T(8,128)(2,1)} %x.3) | copy-start | bytes 393220
  8.8 15.6 %collective-permute-start.16 = (bf16[512,256]{1,0:T(8,128)(2,1)S(1)}, bf16[512,256]{1,0:T(8,128)(2,1)S(1)}, u32[]{:S(2)}, u32[]{:S(2)}) collective-permute-start(bf16[512,256]{1,0:T(8,128)(2,1)S(1)} %get-tuple-element.32.refs_0_), channel_id=1, source_target_pairs={{0,1},{1,2},{2,3},{3,0},{4,5},{5,6},{6,7},{7,4},{8,9},{9,10},{10,1... | collective-permute-start | bytes 786440 | tf_op jit(solution)/shard_map/ppermute | solution.py:44
  10.8 13.6 %collective-permute-start.17 = (bf16[512,256]{1,0:T(8,128)(2,1)S(1)}, bf16[512,256]{1,0:T(8,128)(2,1)S(1)}, u32[]{:S(2)}, u32[]{:S(2)}) collective-permute-start(bf16[512,256]{1,0:T(8,128)(2,1)S(1)} %get-tuple-element.32.refs_0_), channel_id=1, source_target_pairs={{0,3},{1,0},{2,1},{3,2},{4,7},{5,4},{6,5},{7,6},{8,11},{9,8},{10,9... | collective-permute-start | bytes 786440 | tf_op jit(solution)/shard_map/ppermute | solution.py:44
  10.9 13.5 %collective-permute-start.18 = (bf16[512,256]{1,0:T(8,128)(2,1)S(1)}, bf16[512,256]{1,0:T(8,128)(2,1)S(1)}, u32[]{:S(2)}, u32[]{:S(2)}) collective-permute-start(bf16[512,256]{1,0:T(8,128)(2,1)S(1)} %get-tuple-element.32.refs_0_), channel_id=1, source_target_pairs={{0,2},{1,3},{2,0},{3,1},{4,6},{5,7},{6,4},{7,5},{8,10},{9,11},{10,... | collective-permute-start | bytes 786440 | tf_op jit(solution)/shard_map/ppermute | solution.py:44
  24.3 20.5 %copy-start = (bf16[32,2048,128]{2,1,0:T(8,128)(2,1)S(1)}, bf16[32,2048,128]{2,1,0:T(8,128)(2,1)}, u32[]{:S(2)}) copy-start(bf16[32,2048,128]{2,1,0:T(8,128)(2,1)} %get-tuple-element.35.panel) | copy-start | bytes 50331652
  26.7 23.0 %collective-permute-start.19 = (bf16[2048,256]{1,0:T(8,128)(2,1)S(1)}, bf16[2048,256]{1,0:T(8,128)(2,1)S(1)}, u32[]{:S(2)}, u32[]{:S(2)}) collective-permute-start(bf16[2048,256]{1,0:T(8,128)(2,1)S(1)} %back.2), channel_id=1, source_target_pairs={{0,8},{8,0},{16,24},{24,16},{32,40},{40,32},{48,56},{56,48},{64,72... | collective-permute-start | bytes 3145736 | tf_op jit(solution)/shard_map/ppermute | solution.py:35
  26.8 9.9 %collective-permute-start.2 = (bf16[512,256]{1,0:T(8,128)(2,1)S(1)}, bf16[512,256]{1,0:T(8,128)(2,1)S(1)}, u32[]{:S(2)}, u32[]{:S(2)}) collective-permute-start(bf16[512,256]{1,0:T(8,128)(2,1)S(1)} %get-tuple-element.33.refs_0_), channel_id=1, source_target_pairs={{0,16},{8,24},{16,32},{24,40},{32,48},{40,56},{48,0},{56,8},{64,80... | collective-permute-start | bytes 786440 | tf_op jit(solution)/shard_map/ppermute | solution.py:35
  28.4 13.3 %collective-permute-start.3 = (bf16[512,256]{1,0:T(8,128)(2,1)S(1)}, bf16[512,256]{1,0:T(8,128)(2,1)S(1)}, u32[]{:S(2)}, u32[]{:S(2)}) collective-permute-start(bf16[512,256]{1,0:T(8,128)(2,1)S(1)} %get-tuple-element.33.refs_0_), channel_id=1, source_target_pairs={{0,48},{8,56},{16,0},{24,8},{32,16},{40,24},{48,32},{56,40},{64,11... | collective-permute-start | bytes 786440 | tf_op jit(solution)/shard_map/ppermute | solution.py:35
  30.1 13.2 %collective-permute-start.4 = (bf16[512,256]{1,0:T(8,128)(2,1)S(1)}, bf16[512,256]{1,0:T(8,128)(2,1)S(1)}, u32[]{:S(2)}, u32[]{:S(2)}) collective-permute-start(bf16[512,256]{1,0:T(8,128)(2,1)S(1)} %get-tuple-element.33.refs_0_), channel_id=1, source_target_pairs={{0,32},{8,40},{16,48},{24,56},{32,0},{40,8},{48,16},{56,24},{64,96... | collective-permute-start | bytes 786440 | tf_op jit(solution)/shard_map/ppermute | solution.py:35
  31.9 11.4 %collective-permute-start.5 = (bf16[512,256]{1,0:T(8,128)(2,1)S(1)}, bf16[512,256]{1,0:T(8,128)(2,1)S(1)}, u32[]{:S(2)}, u32[]{:S(2)}) collective-permute-start(bf16[512,256]{1,0:T(8,128)(2,1)S(1)} %get-tuple-element.33.refs_0_), channel_id=1, source_target_pairs={{0,8},{8,0},{16,24},{24,16},{32,40},{40,32},{48,56},{56,48},{64,72... | collective-permute-start | bytes 786440 | tf_op jit(solution)/shard_map/ppermute | solution.py:35
  36.7 6.6 %collective-permute-start.6 = (bf16[512,256]{1,0:T(8,128)(2,1)S(1)}, bf16[512,256]{1,0:T(8,128)(2,1)S(1)}, u32[]{:S(2)}, u32[]{:S(2)}) collective-permute-start(bf16[512,256]{1,0:T(8,128)(2,1)S(1)} %collective-permute-done.2.refs_1_), channel_id=1, source_target_pairs={{0,8},{8,0},{16,24},{24,16},{32,40},{40,32},{48,56},{56,48},{64,72... | collective-permute-start | bytes 786440 | tf_op jit(solution)/shard_map/ppermute | solution.py:35
  41.6 1.7 %collective-permute-start.7 = (bf16[512,256]{1,0:T(8,128)(2,1)S(1)}, bf16[512,256]{1,0:T(8,128)(2,1)S(1)}, u32[]{:S(2)}, u32[]{:S(2)}) collective-permute-start(bf16[512,256]{1,0:T(8,128)(2,1)S(1)} %collective-permute-done.3.refs_2_), channel_id=1, source_target_pairs={{0,8},{8,0},{16,24},{24,16},{32,40},{40,32},{48,56},{56,48},{64,72... | collective-permute-start | bytes 786440 | tf_op jit(solution)/shard_map/ppermute | solution.py:35
  43.3 1.5 %collective-permute-start.8 = (bf16[512,256]{1,0:T(8,128)(2,1)S(1)}, bf16[512,256]{1,0:T(8,128)(2,1)S(1)}, u32[]{:S(2)}, u32[]{:S(2)}) collective-permute-start(bf16[512,256]{1,0:T(8,128)(2,1)S(1)} %collective-permute-done.4.refs_3_), channel_id=1, source_target_pairs={{0,8},{8,0},{16,24},{24,16},{32,40},{40,32},{48,56},{56,48},{64,72... | collective-permute-start | bytes 786440 | tf_op jit(solution)/shard_map/ppermute | solution.py:35
  46.7 9.9 %collective-permute-start.12 = (bf16[256,256]{1,0:T(8,128)(2,1)S(1)}, bf16[256,256]{1,0:T(8,128)(2,1)S(1)}, u32[]{:S(2)}, u32[]{:S(2)}) collective-permute-start(bf16[256,256]{1,0:T(8,128)(2,1)S(1)} %get-tuple-element.41), channel_id=1, source_target_pairs={{0,1},{1,2},{2,3},{3,0},{4,5},{5,6},{6,7},{7,4},{8,9},{9,10},{10,1... | collective-permute-start | bytes 393224 | tf_op jit(solution)/shard_map/ppermute | solution.py:44
  50.0 15.7 %collective-permute-start.20 = (bf16[512,256]{1,0:T(8,128)(2,1)S(1)}, bf16[512,256]{1,0:T(8,128)(2,1)S(1)}, u32[]{:S(2)}, u32[]{:S(2)}) collective-permute-start(bf16[512,256]{1,0:T(8,128)(2,1)S(1)} %get-tuple-element.50), channel_id=1, source_target_pairs={{0,16},{8,24},{16,32},{24,40},{32,48},{40,56},{48,0},{56,8},{64,80... | collective-permute-start | bytes 786440 | tf_op jit(solution)/shard_map/ppermute | solution.py:35
  51.2 17.2 %collective-permute-start.21 = (bf16[512,256]{1,0:T(8,128)(2,1)S(1)}, bf16[512,256]{1,0:T(8,128)(2,1)S(1)}, u32[]{:S(2)}, u32[]{:S(2)}) collective-permute-start(bf16[512,256]{1,0:T(8,128)(2,1)S(1)} %get-tuple-element.51), channel_id=1, source_target_pairs={{0,48},{8,56},{16,0},{24,8},{32,16},{40,24},{48,32},{56,40},{64,11... | collective-permute-start | bytes 786440 | tf_op jit(solution)/shard_map/ppermute | solution.py:35
  53.3 16.8 %collective-permute-start.22 = (bf16[512,256]{1,0:T(8,128)(2,1)S(1)}, bf16[512,256]{1,0:T(8,128)(2,1)S(1)}, u32[]{:S(2)}, u32[]{:S(2)}) collective-permute-start(bf16[512,256]{1,0:T(8,128)(2,1)S(1)} %get-tuple-element.52), channel_id=1, source_target_pairs={{0,32},{8,40},{16,48},{24,56},{32,0},{40,8},{48,16},{56,24},{64,96... | collective-permute-start | bytes 786440 | tf_op jit(solution)/shard_map/ppermute | solution.py:35
  53.9 24.2 %copy-start.1 = (bf16[256,1024]{1,0:T(8,128)(2,1)S(1)}, bf16[256,1024]{1,0:T(8,128)(2,1)}, u32[]{:S(2)}) copy-start(bf16[256,1024]{1,0:T(8,128)(2,1)} %refs_8_.1) | copy-start | bytes 1572868
  53.9 24.2 %copy-start.2 = (bf16[1024,256]{1,0:T(8,128)(2,1)S(1)}, bf16[1024,256]{1,0:T(8,128)(2,1)}, u32[]{:S(2)}) copy-start(bf16[1024,256]{1,0:T(8,128)(2,1)} %refs_10_.1) | copy-start | bytes 1572868
  53.9 24.2 %copy-start.4 = (f32[1024]{0:T(1024)S(1)}, f32[1024]{0:T(1024)}, u32[]{:S(2)}) copy-start(f32[1024]{0:T(1024)} %param.15) | copy-start | bytes 12292
  53.9 24.2 %copy-start.5 = (f32[256]{0:T(256)S(1)}, f32[256]{0:T(256)}, u32[]{:S(2)}) copy-start(f32[256]{0:T(256)} %param.17) | copy-start | bytes 3076
  53.9 6.1 %collective-permute-start.13 = (bf16[256,256]{1,0:T(8,128)(2,1)S(1)}, bf16[256,256]{1,0:T(8,128)(2,1)S(1)}, u32[]{:S(2)}, u32[]{:S(2)}) collective-permute-start(bf16[256,256]{1,0:T(8,128)(2,1)S(1)} %get-tuple-element.42), channel_id=1, source_target_pairs={{0,3},{1,0},{2,1},{3,2},{4,7},{5,4},{6,5},{7,6},{8,11},{9,8},{10,9... | collective-permute-start | bytes 393224 | tf_op jit(solution)/shard_map/ppermute | solution.py:44
  56.6 6.7 %collective-permute-start.14 = (bf16[256,256]{1,0:T(8,128)(2,1)S(1)}, bf16[256,256]{1,0:T(8,128)(2,1)S(1)}, u32[]{:S(2)}, u32[]{:S(2)}) collective-permute-start(bf16[256,256]{1,0:T(8,128)(2,1)S(1)} %get-tuple-element.43), channel_id=1, source_target_pairs={{0,2},{1,3},{2,0},{3,1},{4,6},{5,7},{6,4},{7,5},{8,10},{9,11},{10,... | collective-permute-start | bytes 393224 | tf_op jit(solution)/shard_map/ppermute | solution.py:44
  60.0 14.0 %collective-permute-start.10 = (bf16[256,256]{1,0:T(8,128)(2,1)S(1)}, bf16[256,256]{1,0:T(8,128)(2,1)S(1)}, u32[]{:S(2)}, u32[]{:S(2)}) collective-permute-start(bf16[256,256]{1,0:T(8,128)(2,1)S(1)} %get-tuple-element.38), channel_id=1, source_target_pairs={{0,3},{1,0},{2,1},{3,2},{4,7},{5,4},{6,5},{7,6},{8,11},{9,8},{10,9... | collective-permute-start | bytes 393224 | tf_op jit(solution)/shard_map/ppermute | solution.py:44
  63.3 10.7 %collective-permute-start.11 = (bf16[256,256]{1,0:T(8,128)(2,1)S(1)}, bf16[256,256]{1,0:T(8,128)(2,1)S(1)}, u32[]{:S(2)}, u32[]{:S(2)}) collective-permute-start(bf16[256,256]{1,0:T(8,128)(2,1)S(1)} %get-tuple-element.39), channel_id=1, source_target_pairs={{0,2},{1,3},{2,0},{3,1},{4,6},{5,7},{6,4},{7,5},{8,10},{9,11},{10,... | collective-permute-start | bytes 393224 | tf_op jit(solution)/shard_map/ppermute | solution.py:44
  65.8 8.2 %collective-permute-start.9 = (bf16[256,256]{1,0:T(8,128)(2,1)S(1)}, bf16[256,256]{1,0:T(8,128)(2,1)S(1)}, u32[]{:S(2)}, u32[]{:S(2)}) collective-permute-start(bf16[256,256]{1,0:T(8,128)(2,1)S(1)} %get-tuple-element.37), channel_id=1, source_target_pairs={{0,1},{1,2},{2,3},{3,0},{4,5},{5,6},{6,7},{7,4},{8,9},{9,10},{10,1... | collective-permute-start | bytes 393224 | tf_op jit(solution)/shard_map/ppermute | solution.py:44
  68.5 6.5 %collective-permute-start.15 = (bf16[256,256]{1,0:T(8,128)(2,1)S(1)}, bf16[256,256]{1,0:T(8,128)(2,1)S(1)}, u32[]{:S(2)}, u32[]{:S(2)}) collective-permute-start(bf16[256,256]{1,0:T(8,128)(2,1)S(1)} %total.1), channel_id=1, source_target_pairs={{0,4},{1,5},{2,6},{3,7},{4,0},{5,1},{6,2},{7,3},{8,12},{9,13},{10,... | collective-permute-start | bytes 393224 | tf_op jit(solution)/shard_map/ppermute | solution.py:44
  70.3 7.8 %collective-permute-start.23 = (bf16[256,256]{1,0:T(8,128)(2,1)S(1)}, bf16[256,256]{1,0:T(8,128)(2,1)S(1)}, u32[]{:S(2)}, u32[]{:S(2)}) collective-permute-start(bf16[256,256]{1,0:T(8,128)(2,1)S(1)} %get-tuple-element.54), channel_id=1, source_target_pairs={{0,64},{8,72},{16,80},{24,88},{32,96},{40,104},{48,112},{56,120},{... | collective-permute-start | bytes 393224 | tf_op jit(solution)/shard_map/ppermute | solution.py:35
where the time goes:
time: 79.5 us; the launch traced here: 79.4 us
  starting transfers between devices  34 us (43%)
  Pallas kernels  21.8 us (27%)
  waiting for transfers between devices  21.1 us (27%)
  local copies, waits for them, and re-layouts  0.92 us (1%)
  between operations  0.85 us (1%)
    ppermute x11, starting transfers between devices, col_perm(): return lax.ppermute(value, 'col', pairs)  19 us
    ppermute x13, waiting for transfers between devices, row_perm(): return lax.ppermute(value, 'row', pairs)  16.8 us
    ppermute x13, starting transfers between devices, row_perm(): return lax.ppermute(value, 'row', pairs)  15 us
    pallas_call x1, Pallas kernels, dense(): pl.pallas_call(dense_kernel, out_shape=(SDS((COLS, ROWS * T, T), BF), plt...  10.5 us
    pallas_call x3, Pallas kernels, forward(): pl.pallas_call(functools.partial(forward_kernel, targets=targets), out_sh...  4.8 us
    pallas_call x2, Pallas kernels, back(): pl.pallas_call(functools.partial(back_kernel, targets=targets), out_shape...  4.66 us
    ppermute x11, waiting for transfers between devices, col_perm(): return lax.ppermute(value, 'col', pairs)  4.36 us
  transfers between devices with their start and end apart: 24, of which 9 were waited for; matrix products, arithmetic and copies ran while one was open for 1% of the time, Pallas kernels for 23%

commit v1 on v0

--- a/solution.py
+++ b/solution.py
@@ -15,6 +15,7 @@
 CAP = 384
 CHUNKS = 12
 CT = CAP // CHUNKS
+SLOTS = 6
 UNROLL = 16
 HOPS = (0, 1, 3, 2)
 BF = jnp.bfloat16
@@ -64,17 +65,7 @@
     return col_perm(value, lambda y, z: (1 - y, z))
 
 
-def dense_kernel(places, tiles, panel_out, panel_t, held, panel, place_s, sems, place_sem, out_sem):
-    place_copy = pltpu.make_async_copy(places, place_s, place_sem)
-    place_copy.start()
-
-    def fetch(q):
-        part = pl.ds(q * CT, CT)
-        return pltpu.make_async_copy(tiles.at[part], held.at[part], sems.at[q])
-
-    for q in range(CHUNKS):
-        fetch(q).start()
-
+def clear_kernel(panel, panel_t):
     def clear(j, _):
         panel[j] = jnp.zeros((ROWS * T, T), BF)
         return 0
@@ -84,43 +75,72 @@
         return 0
 
     lax.fori_loop(0, COLS, clear, 0)
+    lax.fori_loop(0, ROWS, clear_t, 0)
+
+
+PANELS = (pltpu.VMEM((COLS, ROWS * T, T), BF), pltpu.VMEM((ROWS, COLS * T, T), BF))
+
+
+def cleared():
+    return pl.pallas_call(
+        clear_kernel,
+        out_shape=PANELS,
+        out_specs=(VMEM, VMEM),
+        compiler_params=pltpu.CompilerParams(vmem_limit_bytes=4 * MIB),
+        cost_estimate=pl.CostEstimate(flops=0, bytes_accessed=12 * MIB, transcendentals=0),
+        name="clear",
+    )()
+
+
+def dense_kernel(places, tiles, _, __, panel, panel_t, held, place_s, sems, place_sem):
+    place_copy = pltpu.make_async_copy(places, place_s, place_sem)
+    place_copy.start()
+
+    def fetch(q):
+        part = pl.ds(q * CT, CT)
+        return pltpu.make_async_copy(tiles.at[part], held.at[q % SLOTS], sems.at[q % SLOTS])
+
     place_copy.wait()
     count = place_s[0, CAP]
 
-    def spot(s):
-        at = place_s[0, s]
-        return lax.div(at, COLS), lax.rem(at, COLS)
-
-    def put(s):
-        i, j = spot(s)
-        panel[j, pl.ds(pl.multiple_of(i * T, T), T), :] = held[s]
-
-    def put_t(s):
-        i, j = spot(s)
-        panel_t[i, pl.ds(pl.multiple_of(j * T, T), T), :] = held[s].T
-
-    def each(low, live, step):
-        def many(g, _):
+    def begin(q):
+        @pl.when(q * CT < count)
+        def _():
+            fetch(q).start()
+
+    for q in range(SLOTS):
+        begin(q)
+
+    def place(s, slot, low):
+        spot = place_s[0, s]
+        i = lax.div(spot, COLS)
+        j = lax.rem(spot, COLS)
+        tile = held[slot, s - low]
+        panel[j, pl.ds(pl.multiple_of(i * T, T), T), :] = tile
+        panel_t[i, pl.ds(pl.multiple_of(j * T, T), T), :] = tile.T
+
+    for q in range(CHUNKS):
+        low = q * CT
+        live = jnp.clip(count - low, 0, CT)
+
+        @pl.when(low < count)
+        def _(q=q):
+            fetch(q).wait()
+
+        def many(g, _, q=q, low=low):
             for u in range(UNROLL):
-                step(low + g * UNROLL + u)
+                place(low + g * UNROLL + u, q % SLOTS, low)
             return 0
 
-        def one(s, _):
-            step(s)
+        def one(s, _, q=q, low=low):
+            place(s, q % SLOTS, low)
             return 0
 
         groups = lax.div(live, UNROLL)
         lax.fori_loop(0, groups, many, 0)
         lax.fori_loop(low + groups * UNROLL, low + live, one, 0)
-
-    for q in range(CHUNKS):
-        fetch(q).wait()
-        each(q * CT, jnp.clip(count - q * CT, 0, CT), put)
-    out_copy = pltpu.make_async_copy(panel, panel_out, out_sem)
-    out_copy.start()
-    lax.fori_loop(0, ROWS, clear_t, 0)
-    each(0, count, put_t)
-    out_copy.wait()
+        if q + SLOTS < CHUNKS:
+            begin(q + SLOTS)
 
 
 def slots(tile_row, tile_column, tile_count):
@@ -129,27 +149,23 @@
     return jnp.where(at == CAP, tile_count[0], spots)
 
 
-def dense(tiles, places):
+def dense(tiles, places, panels):
     return pl.pallas_call(
         dense_kernel,
-        out_shape=(
-            SDS((COLS, ROWS * T, T), BF),
-            pltpu.VMEM((ROWS, COLS * T, T), BF),
-        ),
-        in_specs=[HBM, HBM],
-        out_specs=(HBM, VMEM),
+        out_shape=PANELS,
+        in_specs=[HBM, HBM, VMEM, VMEM],
+        out_specs=(VMEM, VMEM),
         scratch_shapes=[
-            pltpu.VMEM((CAP, T, T), BF),
-            pltpu.VMEM((COLS, ROWS * T, T), BF),
+            pltpu.VMEM((SLOTS, CT, T, T), BF),
             pltpu.SMEM((1, CAP + T), jnp.int32),
-            pltpu.SemaphoreType.DMA((CHUNKS,)),
-            pltpu.SemaphoreType.DMA,
+            pltpu.SemaphoreType.DMA((SLOTS,)),
             pltpu.SemaphoreType.DMA,
         ],
-        compiler_params=pltpu.CompilerParams(vmem_limit_bytes=30 * MIB),
+        compiler_params=pltpu.CompilerParams(vmem_limit_bytes=12 * MIB),
         cost_estimate=pl.CostEstimate(flops=0, bytes_accessed=45 * MIB, transcendentals=0),
+        input_output_aliases={2: 0, 3: 1},
         name="dense",
-    )(places, tiles)
+    )(places, tiles, *panels)
 
 
 def row_place():
@@ -370,7 +386,9 @@
 def shards(
     features, adjacency, tile_row, tile_column, tile_count, weight_in, bias_in, weight_out, bias_out
 ):
-    high, low = to_yhi(features), to_ylo(features)
+    high = to_yhi(features)
+    low = to_ylo(features)
+    panels = cleared()
     own_features = stage(features)
     places = slots(tile_row, tile_column, tile_count)
     own_features, places = lax.optimization_barrier((own_features, places))
@@ -381,7 +399,7 @@
         row_pairs.append(to_z(row_pair, d))
 
     places, _ = lax.optimization_barrier((places, (row_pair, col_pair)))
-    panel, panel_t = dense(adjacency[0], places)
+    panel, panel_t = dense(adjacency[0], places, panels)
     col_pairs = col_pairs + [to_core(block) for block in col_pairs]
 
     (to_other,) = back(panel_t, row_pairs, tuple((h, 1) for h in HOPS), True)

time: 79.5 us -> 80 us (level)
  waiting for transfers between devices: 21.1 us -> 25.4 us
  Pallas kernels: 21.8 us -> 18.6 us
    ppermute x11, waiting for transfers between devices: 4.36 us -> 7.86 us  [col_perm(): return lax.ppermute(value, 'col', pairs)]
    pallas_call x1 -> x2, Pallas kernels: 10.5 us -> 7.2 us  [the longest x1 4.37 us: cleared(): pl.pallas_call(clear_kernel, out_shape=PANELS, out_specs=(VMEM, VMEM), co...]
    ppermute x11, starting transfers between devices: 19 us -> 17.7 us  [col_perm(): return lax.ppermute(value, 'col', pairs)]
  transfers between devices with their start and end apart: 24 -> 24, of which waited for: 9 -> 11; matrix products, arithmetic and copies ran while one was open for 1% -> 1% of each run, Pallas kernels for 23% -> 19%
where the time goes in v1:
time: 80 us; the launch traced here: 79.8 us
  starting transfers between devices  33.4 us (42%)
  waiting for transfers between devices  25.4 us (32%)
  Pallas kernels  18.6 us (23%)
  local copies, waits for them, and re-layouts  0.92 us (1%)
  between operations  0.83 us (1%)
    ppermute x11, starting transfers between devices, col_perm(): return lax.ppermute(value, 'col', pairs)  17.7 us
    ppermute x13, waiting for transfers between devices, row_perm(): return lax.ppermute(value, 'row', pairs)  17.5 us
    ppermute x13, starting transfers between devices, row_perm(): return lax.ppermute(value, 'row', pairs)  15.7 us
    ppermute x11, waiting for transfers between devices, col_perm(): return lax.ppermute(value, 'col', pairs)  7.86 us
    pallas_call x3, Pallas kernels, forward(): pl.pallas_call(functools.partial(forward_kernel, targets=targets), out_sh...  4.84 us
    pallas_call x2, Pallas kernels, back(): pl.pallas_call(functools.partial(back_kernel, targets=targets), out_shape...  4.66 us
    pallas_call x1, Pallas kernels, cleared(): pl.pallas_call(clear_kernel, out_shape=PANELS, out_specs=(VMEM, VMEM), co...  4.37 us
    pallas_call x1, Pallas kernels, dense(): pl.pallas_call(dense_kernel, out_shape=PANELS, in_specs=[HBM, HBM, VMEM,...  2.82 us
  transfers between devices with their start and end apart: 24, of which 11 were waited for; matrix products, arithmetic and copies ran while one was open for 1% of the time, Pallas kernels for 19%

profile of v1, /device:TPU:48, one launch (start us, length us, event | category | flops | bytes accessed | tf_op | source)
XLA Modules:
  0.0 79.8 jit_solution(7721448025953514877)
XLA Ops:
  0.3 2.2 %collective-permute-start.1 = (bf16[256,256]{1,0:T(8,128)(2,1)}, bf16[256,256]{1,0:T(8,128)(2,1)S(1)}, u32[]{:S(2)}, u32[]{:S(2)}) collective-permute-start(bf16[256,256]{1,0:T(8,128)(2,1)} %x.3), channel_id=1, source_target_pairs={{0,64},{8,72},{16,80},{24,88},{32,96},{40,104},{48,112},{56,120},{... | collective-permute-start | bytes 393224 | tf_op jit(solution)/shard_map/ppermute | solution.py:36
  3.2 0.9 %copy-done.2 = bf16[256,256]{1,0:T(8,128)(2,1)S(1)} copy-done((bf16[256,256]{1,0:T(8,128)(2,1)S(1)}, bf16[256,256]{1,0:T(8,128)(2,1)}, u32[]{:S(2)}) %copy-start.2) | copy-done | bytes 131096
  4.9 3.1 %collective-permute-done.high = bf16[256,256]{1,0:T(8,128)(2,1)S(1)} collective-permute-done((bf16[256,256]{1,0:T(8,128)(2,1)}, bf16[256,256]{1,0:T(8,128)(2,1)S(1)}, u32[]{:S(2)}, u32[]{:S(2)}) %collective-permute-start) | collective-permute-done | bytes 131104 | tf_op jit(solution)/shard_map/ppermute | solution.py:45
  8.8 2.0 %collective-permute-start.16 = (bf16[512,256]{1,0:T(8,128)(2,1)S(1)}, bf16[512,256]{1,0:T(8,128)(2,1)S(1)}, u32[]{:S(2)}, u32[]{:S(2)}) collective-permute-start(bf16[512,256]{1,0:T(8,128)(2,1)S(1)} %get-tuple-element.34.refs_0_), channel_id=1, source_target_pairs={{0,1},{1,2},{2,3},{3,0},{4,5},{5,6},{6,7},{7,4},{8,9},{9,10},{10,1... | collective-permute-start | bytes 786440 | tf_op jit(solution)/shard_map/ppermute | solution.py:45
  10.9 3.0 %collective-permute-start.18 = (bf16[512,256]{1,0:T(8,128)(2,1)S(1)}, bf16[512,256]{1,0:T(8,128)(2,1)S(1)}, u32[]{:S(2)}, u32[]{:S(2)}) collective-permute-start(bf16[512,256]{1,0:T(8,128)(2,1)S(1)} %get-tuple-element.34.refs_0_), channel_id=1, source_target_pairs={{0,2},{1,3},{2,0},{3,1},{4,6},{5,7},{6,4},{7,5},{8,10},{9,11},{10,... | collective-permute-start | bytes 786440 | tf_op jit(solution)/shard_map/ppermute | solution.py:45
  13.9 4.4 %clear.1 = (bf16[32,2048,128]{2,1,0:T(8,128)(2,1)S(1)}, bf16[16,4096,128]{2,1,0:T(8,128)(2,1)S(1)}) custom-call(), custom_call_target="tpu_custom_call" | custom-call | bytes 12582912 | tf_op jit(solution)/shard_map/clear/pallas_call | solution.py:85
  18.2 2.8 %dense.1 = (bf16[32,2048,128]{2,1,0:T(8,128)(2,1)S(1)}, bf16[16,4096,128]{2,1,0:T(8,128)(2,1)S(1)}) custom-call(s32[1,512]{1,0:T(1,128)S(1)} %compare_select_fusion.places, bf16[384,128,128]{2,1,0:T(8,128)(2,1)} %bitcast.7, bf16[32,2048,128]{2,1,0:T(8,128)(2,1)S(1)} %get-tuple-element.37._, ...), custom_call_target="tpu_custom_call", output_to_operand_aliasing={{0}: (2, {}), {1}: (3, {})} | custom-call | bytes 47185920 | tf_op jit(solution)/shard_map/dense/pallas_call | solution.py:153
  21.1 3.2 %collective-permute-done.18.refs_3_ = bf16[512,256]{1,0:T(8,128)(2,1)S(1)} collective-permute-done((bf16[512,256]{1,0:T(8,128)(2,1)S(1)}, bf16[512,256]{1,0:T(8,128)(2,1)S(1)}, u32[]{:S(2)}, u32[]{:S(2)}) %collective-permute-start.18) | collective-permute-done | bytes 262176 | tf_op jit(solution)/shard_map/ppermute | solution.py:45
  24.4 2.3 %back.2 = bf16[2048,256]{1,0:T(8,128)(2,1)S(1)} custom-call(bf16[16,4096,128]{2,1,0:T(8,128)(2,1)S(1)} %get-tuple-element.48.panel_t, bf16[512,256]{1,0:T(8,128)(2,1)S(1)} %get-tuple-element.34.refs_0_, bf16[512,256]{1,0:T(8,128)(2,1)S(1)} %collective-permute-done.16.refs_1_, bf16[512,256]{1,0:T(8,128)(2,1)S(1)} %collective-permute-done.17.refs_2_, ...), custom_call_target="tpu_custom_call" | custom-call | flops 2147483648 | bytes 4194304 | tf_op jit(solution)/shard_map/back/pallas_call | solution.py:228
  26.8 1.6 %collective-permute-start.2 = (bf16[512,256]{1,0:T(8,128)(2,1)S(1)}, bf16[512,256]{1,0:T(8,128)(2,1)S(1)}, u32[]{:S(2)}, u32[]{:S(2)}) collective-permute-start(bf16[512,256]{1,0:T(8,128)(2,1)S(1)} %get-tuple-element.35.refs_0_), channel_id=1, source_target_pairs={{0,16},{8,24},{16,32},{24,40},{32,48},{40,56},{48,0},{56,8},{64,80... | collective-permute-start | bytes 786440 | tf_op jit(solution)/shard_map/ppermute | solution.py:36
  28.4 1.7 %collective-permute-start.3 = (bf16[512,256]{1,0:T(8,128)(2,1)S(1)}, bf16[512,256]{1,0:T(8,128)(2,1)S(1)}, u32[]{:S(2)}, u32[]{:S(2)}) collective-permute-start(bf16[512,256]{1,0:T(8,128)(2,1)S(1)} %get-tuple-element.35.refs_0_), channel_id=1, source_target_pairs={{0,48},{8,56},{16,0},{24,8},{32,16},{40,24},{48,32},{56,40},{64,11... | collective-permute-start | bytes 786440 | tf_op jit(solution)/shard_map/ppermute | solution.py:36
  30.1 1.8 %collective-permute-start.4 = (bf16[512,256]{1,0:T(8,128)(2,1)S(1)}, bf16[512,256]{1,0:T(8,128)(2,1)S(1)}, u32[]{:S(2)}, u32[]{:S(2)}) collective-permute-start(bf16[512,256]{1,0:T(8,128)(2,1)S(1)} %get-tuple-element.35.refs_0_), channel_id=1, source_target_pairs={{0,32},{8,40},{16,48},{24,56},{32,0},{40,8},{48,16},{56,24},{64,96... | collective-permute-start | bytes 786440 | tf_op jit(solution)/shard_map/ppermute | solution.py:36
  31.9 4.8 %collective-permute-done.2.refs_1_ = bf16[512,256]{1,0:T(8,128)(2,1)S(1)} collective-permute-done((bf16[512,256]{1,0:T(8,128)(2,1)S(1)}, bf16[512,256]{1,0:T(8,128)(2,1)S(1)}, u32[]{:S(2)}, u32[]{:S(2)}) %collective-permute-start.2) | collective-permute-done | bytes 262176 | tf_op jit(solution)/shard_map/ppermute | solution.py:36
  36.7 4.9 %collective-permute-done.3.refs_2_ = bf16[512,256]{1,0:T(8,128)(2,1)S(1)} collective-permute-done((bf16[512,256]{1,0:T(8,128)(2,1)S(1)}, bf16[512,256]{1,0:T(8,128)(2,1)S(1)}, u32[]{:S(2)}, u32[]{:S(2)}) %collective-permute-start.3) | collective-permute-done | bytes 262176 | tf_op jit(solution)/shard_map/ppermute | solution.py:36
  41.6 1.7 %collective-permute-done.4.refs_3_ = bf16[512,256]{1,0:T(8,128)(2,1)S(1)} collective-permute-done((bf16[512,256]{1,0:T(8,128)(2,1)S(1)}, bf16[512,256]{1,0:T(8,128)(2,1)S(1)}, u32[]{:S(2)}, u32[]{:S(2)}) %collective-permute-start.4) | collective-permute-done | bytes 262176 | tf_op jit(solution)/shard_map/ppermute | solution.py:36
  43.3 1.5 %collective-permute-done.8.refs_7_ = bf16[512,256]{1,0:T(8,128)(2,1)S(1)} collective-permute-done((bf16[512,256]{1,0:T(8,128)(2,1)S(1)}, bf16[512,256]{1,0:T(8,128)(2,1)S(1)}, u32[]{:S(2)}, u32[]{:S(2)}) %collective-permute-start.8) | collective-permute-done | bytes 262176 | tf_op jit(solution)/shard_map/ppermute | solution.py:36
  44.8 1.8 %forward.5 = (bf16[256,256]{1,0:T(8,128)(2,1)S(1)}, bf16[256,256]{1,0:T(8,128)(2,1)S(1)}, bf16[256,256]{1,0:T(8,128)(2,1)S(1)}) custom-call(bf16[32,2048,128]{2,1,0:T(8,128)(2,1)S(1)} %get-tuple-element.39.panel, bf16[512,256]{1,0:T(8,128)(2,1)S(1)} %get-tuple-element.35.refs_0_, bf16[512,256]{1,0:T(8,128)(2,1)S(1)} %collective-permute-done.2.refs_1_, ...), custom_call_target="tpu_custom_call" | custom-call | flops 1610612736 | bytes 1572864 | tf_op jit(solution)/shard_map/forward/pallas_call | solution.py:260
  46.9 2.3 %back.3 = (bf16[512,256]{1,0:T(8,128)(2,1)S(1)}, bf16[512,256]{1,0:T(8,128)(2,1)S(1)}, bf16[512,256]{1,0:T(8,128)(2,1)S(1)}, bf16[512,256]{1,0:T(8,128)(2,1)S(1)}) custom-call(bf16[16,4096,128]{2,1,0:T(8,128)(2,1)S(1)} %get-tuple-element.48.panel_t, bf16[512,256]{1,0:T(8,128)(2,1)S(1)} %get-tuple-element.34.refs_0_, ...), custom_call_target="tpu_custom_call" | custom-call | flops 2147483648 | bytes 4194304 | tf_op jit(solution)/shard_map/back/pallas_call | solution.py:228
  49.5 1.2 %collective-permute-start.20 = (bf16[512,256]{1,0:T(8,128)(2,1)S(1)}, bf16[512,256]{1,0:T(8,128)(2,1)S(1)}, u32[]{:S(2)}, u32[]{:S(2)}) collective-permute-start(bf16[512,256]{1,0:T(8,128)(2,1)S(1)} %get-tuple-element.54), channel_id=1, source_target_pairs={{0,16},{8,24},{16,32},{24,40},{32,48},{40,56},{48,0},{56,8},{64,80... | collective-permute-start | bytes 786440 | tf_op jit(solution)/shard_map/ppermute | solution.py:36
  50.7 2.1 %collective-permute-start.21 = (bf16[512,256]{1,0:T(8,128)(2,1)S(1)}, bf16[512,256]{1,0:T(8,128)(2,1)S(1)}, u32[]{:S(2)}, u32[]{:S(2)}) collective-permute-start(bf16[512,256]{1,0:T(8,128)(2,1)S(1)} %get-tuple-element.55), channel_id=1, source_target_pairs={{0,48},{8,56},{16,0},{24,8},{32,16},{40,24},{48,32},{56,40},{64,11... | collective-permute-start | bytes 786440 | tf_op jit(solution)/shard_map/ppermute | solution.py:36
  53.4 2.1 %collective-permute-start.13 = (bf16[256,256]{1,0:T(8,128)(2,1)S(1)}, bf16[256,256]{1,0:T(8,128)(2,1)S(1)}, u32[]{:S(2)}, u32[]{:S(2)}) collective-permute-start(bf16[256,256]{1,0:T(8,128)(2,1)S(1)} %get-tuple-element.46), channel_id=1, source_target_pairs={{0,3},{1,0},{2,1},{3,2},{4,7},{5,4},{6,5},{7,6},{8,11},{9,8},{10,9... | collective-permute-start | bytes 393224 | tf_op jit(solution)/shard_map/ppermute | solution.py:45
  55.5 1.2 %forward.3 = (f32[256,256]{1,0:T(8,128)S(1)}, f32[256,256]{1,0:T(8,128)S(1)}) custom-call(bf16[32,2048,128]{2,1,0:T(8,128)(2,1)S(1)} %get-tuple-element.39.panel, bf16[512,256]{1,0:T(8,128)(2,1)S(1)} %get-tuple-element.35.refs_0_, bf16[512,256]{1,0:T(8,128)(2,1)S(1)} %collective-permute-done.2.refs_1_, bf16[512,256]{1,0:T(8,128)(2,1)S(1)} %collective-permute-done.3.refs_2_, ...), custom_call_target="tpu_custom_call" | custom-call | flops 1073741824 | bytes 1048576 | tf_op jit(solution)/shard_map/forward/pallas_call | solution.py:260
  56.8 1.7 %collective-permute-start.14 = (bf16[256,256]{1,0:T(8,128)(2,1)S(1)}, bf16[256,256]{1,0:T(8,128)(2,1)S(1)}, u32[]{:S(2)}, u32[]{:S(2)}) collective-permute-start(bf16[256,256]{1,0:T(8,128)(2,1)S(1)} %get-tuple-element.47), channel_id=1, source_target_pairs={{0,2},{1,3},{2,0},{3,1},{4,6},{5,7},{6,4},{7,5},{8,10},{9,11},{10,... | collective-permute-start | bytes 393224 | tf_op jit(solution)/shard_map/ppermute | solution.py:45
  58.4 1.8 %forward.4 = (bf16[256,256]{1,0:T(8,128)(2,1)S(1)}, bf16[256,256]{1,0:T(8,128)(2,1)S(1)}, bf16[256,256]{1,0:T(8,128)(2,1)S(1)}) custom-call(bf16[32,2048,128]{2,1,0:T(8,128)(2,1)S(1)} %get-tuple-element.39.panel, bf16[512,256]{1,0:T(8,128)(2,1)S(1)} %get-tuple-element.35.refs_0_, bf16[512,256]{1,0:T(8,128)(2,1)S(1)} %collective-permute-done.2.refs_1_, ...), custom_call_target="tpu_custom_call" | custom-call | flops 1610612736 | bytes 1572864 | tf_op jit(solution)/shard_map/forward/pallas_call | solution.py:260
  60.2 2.2 %collective-permute-start.10 = (bf16[256,256]{1,0:T(8,128)(2,1)S(1)}, bf16[256,256]{1,0:T(8,128)(2,1)S(1)}, u32[]{:S(2)}, u32[]{:S(2)}) collective-permute-start(bf16[256,256]{1,0:T(8,128)(2,1)S(1)} %get-tuple-element.42), channel_id=1, source_target_pairs={{0,3},{1,0},{2,1},{3,2},{4,7},{5,4},{6,5},{7,6},{8,11},{9,8},{10,9... | collective-permute-start | bytes 393224 | tf_op jit(solution)/shard_map/ppermute | solution.py:45
  62.4 1.2 %collective-permute-done.14.refs_3_ = bf16[256,256]{1,0:T(8,128)(2,1)S(1)} collective-permute-done((bf16[256,256]{1,0:T(8,128)(2,1)S(1)}, bf16[256,256]{1,0:T(8,128)(2,1)S(1)}, u32[]{:S(2)}, u32[]{:S(2)}) %collective-permute-start.14) | collective-permute-done | bytes 131104 | tf_op jit(solution)/shard_map/ppermute | solution.py:45
  63.7 2.1 %collective-permute-start.11 = (bf16[256,256]{1,0:T(8,128)(2,1)S(1)}, bf16[256,256]{1,0:T(8,128)(2,1)S(1)}, u32[]{:S(2)}, u32[]{:S(2)}) collective-permute-start(bf16[256,256]{1,0:T(8,128)(2,1)S(1)} %get-tuple-element.43), channel_id=1, source_target_pairs={{0,2},{1,3},{2,0},{3,1},{4,6},{5,7},{6,4},{7,5},{8,10},{9,11},{10,... | collective-permute-start | bytes 393224 | tf_op jit(solution)/shard_map/ppermute | solution.py:45
  65.8 2.3 %collective-permute-start.9 = (bf16[256,256]{1,0:T(8,128)(2,1)S(1)}, bf16[256,256]{1,0:T(8,128)(2,1)S(1)}, u32[]{:S(2)}, u32[]{:S(2)}) collective-permute-start(bf16[256,256]{1,0:T(8,128)(2,1)S(1)} %get-tuple-element.41), channel_id=1, source_target_pairs={{0,1},{1,2},{2,3},{3,0},{4,5},{5,6},{6,7},{7,4},{8,9},{9,10},{10,1... | collective-permute-start | bytes 393224 | tf_op jit(solution)/shard_map/ppermute | solution.py:45
  68.1 1.7 %collective-permute-start.15 = (bf16[256,256]{1,0:T(8,128)(2,1)S(1)}, bf16[256,256]{1,0:T(8,128)(2,1)S(1)}, u32[]{:S(2)}, u32[]{:S(2)}) collective-permute-start(bf16[256,256]{1,0:T(8,128)(2,1)S(1)} %total.1), channel_id=1, source_target_pairs={{0,4},{1,5},{2,6},{3,7},{4,0},{5,1},{6,2},{7,3},{8,12},{9,13},{10,... | collective-permute-start | bytes 393224 | tf_op jit(solution)/shard_map/ppermute | solution.py:45
  69.9 4.5 %collective-permute-start.23 = (bf16[256,256]{1,0:T(8,128)(2,1)S(1)}, bf16[256,256]{1,0:T(8,128)(2,1)S(1)}, u32[]{:S(2)}, u32[]{:S(2)}) collective-permute-start(bf16[256,256]{1,0:T(8,128)(2,1)S(1)} %get-tuple-element.58), channel_id=1, source_target_pairs={{0,64},{8,72},{16,80},{24,88},{32,96},{40,104},{48,112},{56,120},{... | collective-permute-start | bytes 393224 | tf_op jit(solution)/shard_map/ppermute | solution.py:36
  74.6 3.9 %collective-permute-done.23.refs_7_ = bf16[256,256]{1,0:T(8,128)(2,1)S(1)} collective-permute-done((bf16[256,256]{1,0:T(8,128)(2,1)S(1)}, bf16[256,256]{1,0:T(8,128)(2,1)S(1)}, u32[]{:S(2)}, u32[]{:S(2)}) %collective-permute-start.23) | collective-permute-done | bytes 131104 | tf_op jit(solution)/shard_map/ppermute | solution.py:36
  78.6 1.3 %update.1 = bf16[256,256]{1,0:T(8,128)(2,1)} custom-call(bf16[256,256]{1,0:T(8,128)(2,1)S(1)} %stage.1.x.refs_0_, f32[256,256]{1,0:T(8,128)S(1)} %get-tuple-element.40.refs_1_, bf16[256,256]{1,0:T(8,128)(2,1)S(1)} %collective-permute-done.9.refs_2_, bf16[256,256]{1,0:T(8,128)(2,1)S(1)} %collective-permute-done.10.refs_3_, ...), custom_call_target="tpu_custom_call" | custom-call | tf_op jit(solution)/shard_map/update/pallas_call | solution.py:376
  (41 shorter events, 3.7 us)
Async XLA Ops:
  0.0 8.1 %collective-permute-start = (bf16[256,256]{1,0:T(8,128)(2,1)}, bf16[256,256]{1,0:T(8,128)(2,1)S(1)}, u32[]{:S(2)}, u32[]{:S(2)}) collective-permute-start(bf16[256,256]{1,0:T(8,128)(2,1)} %x.3), channel_id=1, source_target_pairs={{0,4},{1,5},{2,6},{3,7},{4,0},{5,1},{6,2},{7,3},{8,12},{9,13},{10,... | collective-permute-start | bytes 393224 | tf_op jit(solution)/shard_map/ppermute | solution.py:45
  0.3 8.4 %collective-permute-start.1 = (bf16[256,256]{1,0:T(8,128)(2,1)}, bf16[256,256]{1,0:T(8,128)(2,1)S(1)}, u32[]{:S(2)}, u32[]{:S(2)}) collective-permute-start(bf16[256,256]{1,0:T(8,128)(2,1)} %x.3), channel_id=1, source_target_pairs={{0,64},{8,72},{16,80},{24,88},{32,96},{40,104},{48,112},{56,120},{... | collective-permute-start | bytes 393224 | tf_op jit(solution)/shard_map/ppermute | solution.py:36
  3.2 0.9 %copy-start.2 = (bf16[256,256]{1,0:T(8,128)(2,1)S(1)}, bf16[256,256]{1,0:T(8,128)(2,1)}, u32[]{:S(2)}) copy-start(bf16[256,256]{1,0:T(8,128)(2,1)} %x.3) | copy-start | bytes 393220
  8.8 12.3 %collective-permute-start.16 = (bf16[512,256]{1,0:T(8,128)(2,1)S(1)}, bf16[512,256]{1,0:T(8,128)(2,1)S(1)}, u32[]{:S(2)}, u32[]{:S(2)}) collective-permute-start(bf16[512,256]{1,0:T(8,128)(2,1)S(1)} %get-tuple-element.34.refs_0_), channel_id=1, source_target_pairs={{0,1},{1,2},{2,3},{3,0},{4,5},{5,6},{6,7},{7,4},{8,9},{9,10},{10,1... | collective-permute-start | bytes 786440 | tf_op jit(solution)/shard_map/ppermute | solution.py:45
  10.8 10.4 %collective-permute-start.17 = (bf16[512,256]{1,0:T(8,128)(2,1)S(1)}, bf16[512,256]{1,0:T(8,128)(2,1)S(1)}, u32[]{:S(2)}, u32[]{:S(2)}) collective-permute-start(bf16[512,256]{1,0:T(8,128)(2,1)S(1)} %get-tuple-element.34.refs_0_), channel_id=1, source_target_pairs={{0,3},{1,0},{2,1},{3,2},{4,7},{5,4},{6,5},{7,6},{8,11},{9,8},{10,9... | collective-permute-start | bytes 786440 | tf_op jit(solution)/shard_map/ppermute | solution.py:45
  10.9 13.5 %collective-permute-start.18 = (bf16[512,256]{1,0:T(8,128)(2,1)S(1)}, bf16[512,256]{1,0:T(8,128)(2,1)S(1)}, u32[]{:S(2)}, u32[]{:S(2)}) collective-permute-start(bf16[512,256]{1,0:T(8,128)(2,1)S(1)} %get-tuple-element.34.refs_0_), channel_id=1, source_target_pairs={{0,2},{1,3},{2,0},{3,1},{4,6},{5,7},{6,4},{7,5},{8,10},{9,11},{10,... | collective-permute-start | bytes 786440 | tf_op jit(solution)/shard_map/ppermute | solution.py:45
  26.7 22.6 %collective-permute-start.19 = (bf16[2048,256]{1,0:T(8,128)(2,1)S(1)}, bf16[2048,256]{1,0:T(8,128)(2,1)S(1)}, u32[]{:S(2)}, u32[]{:S(2)}) collective-permute-start(bf16[2048,256]{1,0:T(8,128)(2,1)S(1)} %back.2), channel_id=1, source_target_pairs={{0,8},{8,0},{16,24},{24,16},{32,40},{40,32},{48,56},{56,48},{64,72... | collective-permute-start | bytes 3145736 | tf_op jit(solution)/shard_map/ppermute | solution.py:36
  26.8 9.9 %collective-permute-start.2 = (bf16[512,256]{1,0:T(8,128)(2,1)S(1)}, bf16[512,256]{1,0:T(8,128)(2,1)S(1)}, u32[]{:S(2)}, u32[]{:S(2)}) collective-permute-start(bf16[512,256]{1,0:T(8,128)(2,1)S(1)} %get-tuple-element.35.refs_0_), channel_id=1, source_target_pairs={{0,16},{8,24},{16,32},{24,40},{32,48},{40,56},{48,0},{56,8},{64,80... | collective-permute-start | bytes 786440 | tf_op jit(solution)/shard_map/ppermute | solution.py:36
  28.4 13.3 %collective-permute-start.3 = (bf16[512,256]{1,0:T(8,128)(2,1)S(1)}, bf16[512,256]{1,0:T(8,128)(2,1)S(1)}, u32[]{:S(2)}, u32[]{:S(2)}) collective-permute-start(bf16[512,256]{1,0:T(8,128)(2,1)S(1)} %get-tuple-element.35.refs_0_), channel_id=1, source_target_pairs={{0,48},{8,56},{16,0},{24,8},{32,16},{40,24},{48,32},{56,40},{64,11... | collective-permute-start | bytes 786440 | tf_op jit(solution)/shard_map/ppermute | solution.py:36
  30.1 13.2 %collective-permute-start.4 = (bf16[512,256]{1,0:T(8,128)(2,1)S(1)}, bf16[512,256]{1,0:T(8,128)(2,1)S(1)}, u32[]{:S(2)}, u32[]{:S(2)}) collective-permute-start(bf16[512,256]{1,0:T(8,128)(2,1)S(1)} %get-tuple-element.35.refs_0_), channel_id=1, source_target_pairs={{0,32},{8,40},{16,48},{24,56},{32,0},{40,8},{48,16},{56,24},{64,96... | collective-permute-start | bytes 786440 | tf_op jit(solution)/shard_map/ppermute | solution.py:36
  31.9 11.4 %collective-permute-start.5 = (bf16[512,256]{1,0:T(8,128)(2,1)S(1)}, bf16[512,256]{1,0:T(8,128)(2,1)S(1)}, u32[]{:S(2)}, u32[]{:S(2)}) collective-permute-start(bf16[512,256]{1,0:T(8,128)(2,1)S(1)} %get-tuple-element.35.refs_0_), channel_id=1, source_target_pairs={{0,8},{8,0},{16,24},{24,16},{32,40},{40,32},{48,56},{56,48},{64,72... | collective-permute-start | bytes 786440 | tf_op jit(solution)/shard_map/ppermute | solution.py:36
  36.7 6.6 %collective-permute-start.6 = (bf16[512,256]{1,0:T(8,128)(2,1)S(1)}, bf16[512,256]{1,0:T(8,128)(2,1)S(1)}, u32[]{:S(2)}, u32[]{:S(2)}) collective-permute-start(bf16[512,256]{1,0:T(8,128)(2,1)S(1)} %collective-permute-done.2.refs_1_), channel_id=1, source_target_pairs={{0,8},{8,0},{16,24},{24,16},{32,40},{40,32},{48,56},{56,48},{64,72... | collective-permute-start | bytes 786440 | tf_op jit(solution)/shard_map/ppermute | solution.py:36
  41.6 1.7 %collective-permute-start.7 = (bf16[512,256]{1,0:T(8,128)(2,1)S(1)}, bf16[512,256]{1,0:T(8,128)(2,1)S(1)}, u32[]{:S(2)}, u32[]{:S(2)}) collective-permute-start(bf16[512,256]{1,0:T(8,128)(2,1)S(1)} %collective-permute-done.3.refs_2_), channel_id=1, source_target_pairs={{0,8},{8,0},{16,24},{24,16},{32,40},{40,32},{48,56},{56,48},{64,72... | collective-permute-start | bytes 786440 | tf_op jit(solution)/shard_map/ppermute | solution.py:36
  43.3 1.5 %collective-permute-start.8 = (bf16[512,256]{1,0:T(8,128)(2,1)S(1)}, bf16[512,256]{1,0:T(8,128)(2,1)S(1)}, u32[]{:S(2)}, u32[]{:S(2)}) collective-permute-start(bf16[512,256]{1,0:T(8,128)(2,1)S(1)} %collective-permute-done.4.refs_3_), channel_id=1, source_target_pairs={{0,8},{8,0},{16,24},{24,16},{32,40},{40,32},{48,56},{56,48},{64,72... | collective-permute-start | bytes 786440 | tf_op jit(solution)/shard_map/ppermute | solution.py:36
  46.7 10.1 %collective-permute-start.12 = (bf16[256,256]{1,0:T(8,128)(2,1)S(1)}, bf16[256,256]{1,0:T(8,128)(2,1)S(1)}, u32[]{:S(2)}, u32[]{:S(2)}) collective-permute-start(bf16[256,256]{1,0:T(8,128)(2,1)S(1)} %get-tuple-element.45), channel_id=1, source_target_pairs={{0,1},{1,2},{2,3},{3,0},{4,5},{5,6},{6,7},{7,4},{8,9},{9,10},{10,1... | collective-permute-start | bytes 393224 | tf_op jit(solution)/shard_map/ppermute | solution.py:45
  49.5 16.3 %collective-permute-start.20 = (bf16[512,256]{1,0:T(8,128)(2,1)S(1)}, bf16[512,256]{1,0:T(8,128)(2,1)S(1)}, u32[]{:S(2)}, u32[]{:S(2)}) collective-permute-start(bf16[512,256]{1,0:T(8,128)(2,1)S(1)} %get-tuple-element.54), channel_id=1, source_target_pairs={{0,16},{8,24},{16,32},{24,40},{32,48},{40,56},{48,0},{56,8},{64,80... | collective-permute-start | bytes 786440 | tf_op jit(solution)/shard_map/ppermute | solution.py:36
  50.7 17.4 %collective-permute-start.21 = (bf16[512,256]{1,0:T(8,128)(2,1)S(1)}, bf16[512,256]{1,0:T(8,128)(2,1)S(1)}, u32[]{:S(2)}, u32[]{:S(2)}) collective-permute-start(bf16[512,256]{1,0:T(8,128)(2,1)S(1)} %get-tuple-element.55), channel_id=1, source_target_pairs={{0,48},{8,56},{16,0},{24,8},{32,16},{40,24},{48,32},{56,40},{64,11... | collective-permute-start | bytes 786440 | tf_op jit(solution)/shard_map/ppermute | solution.py:36
  52.8 17.0 %collective-permute-start.22 = (bf16[512,256]{1,0:T(8,128)(2,1)S(1)}, bf16[512,256]{1,0:T(8,128)(2,1)S(1)}, u32[]{:S(2)}, u32[]{:S(2)}) collective-permute-start(bf16[512,256]{1,0:T(8,128)(2,1)S(1)} %get-tuple-element.56), channel_id=1, source_target_pairs={{0,32},{8,40},{16,48},{24,56},{32,0},{40,8},{48,16},{56,24},{64,96... | collective-permute-start | bytes 786440 | tf_op jit(solution)/shard_map/ppermute | solution.py:36
  53.4 25.1 %copy-start = (bf16[256,1024]{1,0:T(8,128)(2,1)S(1)}, bf16[256,1024]{1,0:T(8,128)(2,1)}, u32[]{:S(2)}) copy-start(bf16[256,1024]{1,0:T(8,128)(2,1)} %refs_8_.1) | copy-start | bytes 1572868
  53.4 25.1 %copy-start.1 = (bf16[1024,256]{1,0:T(8,128)(2,1)S(1)}, bf16[1024,256]{1,0:T(8,128)(2,1)}, u32[]{:S(2)}) copy-start(bf16[1024,256]{1,0:T(8,128)(2,1)} %refs_10_.1) | copy-start | bytes 1572868
  53.4 25.1 %copy-start.3 = (f32[1024]{0:T(1024)S(1)}, f32[1024]{0:T(1024)}, u32[]{:S(2)}) copy-start(f32[1024]{0:T(1024)} %param.15) | copy-start | bytes 12292
  53.4 25.1 %copy-start.4 = (f32[256]{0:T(256)S(1)}, f32[256]{0:T(256)}, u32[]{:S(2)}) copy-start(f32[256]{0:T(256)} %param.17) | copy-start | bytes 3076
  53.4 6.8 %collective-permute-start.13 = (bf16[256,256]{1,0:T(8,128)(2,1)S(1)}, bf16[256,256]{1,0:T(8,128)(2,1)S(1)}, u32[]{:S(2)}, u32[]{:S(2)}) collective-permute-start(bf16[256,256]{1,0:T(8,128)(2,1)S(1)} %get-tuple-element.46), channel_id=1, source_target_pairs={{0,3},{1,0},{2,1},{3,2},{4,7},{5,4},{6,5},{7,6},{8,11},{9,8},{10,9... | collective-permute-start | bytes 393224 | tf_op jit(solution)/shard_map/ppermute | solution.py:45
  56.8 6.9 %collective-permute-start.14 = (bf16[256,256]{1,0:T(8,128)(2,1)S(1)}, bf16[256,256]{1,0:T(8,128)(2,1)S(1)}, u32[]{:S(2)}, u32[]{:S(2)}) collective-permute-start(bf16[256,256]{1,0:T(8,128)(2,1)S(1)} %get-tuple-element.47), channel_id=1, source_target_pairs={{0,2},{1,3},{2,0},{3,1},{4,6},{5,7},{6,4},{7,5},{8,10},{9,11},{10,... | collective-permute-start | bytes 393224 | tf_op jit(solution)/shard_map/ppermute | solution.py:45
  60.2 14.2 %collective-permute-start.10 = (bf16[256,256]{1,0:T(8,128)(2,1)S(1)}, bf16[256,256]{1,0:T(8,128)(2,1)S(1)}, u32[]{:S(2)}, u32[]{:S(2)}) collective-permute-start(bf16[256,256]{1,0:T(8,128)(2,1)S(1)} %get-tuple-element.42), channel_id=1, source_target_pairs={{0,3},{1,0},{2,1},{3,2},{4,7},{5,4},{6,5},{7,6},{8,11},{9,8},{10,9... | collective-permute-start | bytes 393224 | tf_op jit(solution)/shard_map/ppermute | solution.py:45
  63.7 10.7 %collective-permute-start.11 = (bf16[256,256]{1,0:T(8,128)(2,1)S(1)}, bf16[256,256]{1,0:T(8,128)(2,1)S(1)}, u32[]{:S(2)}, u32[]{:S(2)}) collective-permute-start(bf16[256,256]{1,0:T(8,128)(2,1)S(1)} %get-tuple-element.43), channel_id=1, source_target_pairs={{0,2},{1,3},{2,0},{3,1},{4,6},{5,7},{6,4},{7,5},{8,10},{9,11},{10,... | collective-permute-start | bytes 393224 | tf_op jit(solution)/shard_map/ppermute | solution.py:45
  65.8 8.6 %collective-permute-start.9 = (bf16[256,256]{1,0:T(8,128)(2,1)S(1)}, bf16[256,256]{1,0:T(8,128)(2,1)S(1)}, u32[]{:S(2)}, u32[]{:S(2)}) collective-permute-start(bf16[256,256]{1,0:T(8,128)(2,1)S(1)} %get-tuple-element.41), channel_id=1, source_target_pairs={{0,1},{1,2},{2,3},{3,0},{4,5},{5,6},{6,7},{7,4},{8,9},{9,10},{10,1... | collective-permute-start | bytes 393224 | tf_op jit(solution)/shard_map/ppermute | solution.py:45
  68.1 6.5 %collective-permute-start.15 = (bf16[256,256]{1,0:T(8,128)(2,1)S(1)}, bf16[256,256]{1,0:T(8,128)(2,1)S(1)}, u32[]{:S(2)}, u32[]{:S(2)}) collective-permute-start(bf16[256,256]{1,0:T(8,128)(2,1)S(1)} %total.1), channel_id=1, source_target_pairs={{0,4},{1,5},{2,6},{3,7},{4,0},{5,1},{6,2},{7,3},{8,12},{9,13},{10,... | collective-permute-start | bytes 393224 | tf_op jit(solution)/shard_map/ppermute | solution.py:45
  69.9 8.6 %collective-permute-start.23 = (bf16[256,256]{1,0:T(8,128)(2,1)S(1)}, bf16[256,256]{1,0:T(8,128)(2,1)S(1)}, u32[]{:S(2)}, u32[]{:S(2)}) collective-permute-start(bf16[256,256]{1,0:T(8,128)(2,1)S(1)} %get-tuple-element.58), channel_id=1, source_target_pairs={{0,64},{8,72},{16,80},{24,88},{32,96},{40,104},{48,112},{56,120},{... | collective-permute-start | bytes 393224 | tf_op jit(solution)/shard_map/ppermute | solution.py:36

commit v2 on v1

--- a/solution.py
+++ b/solution.py
@@ -65,7 +65,7 @@
     return col_perm(value, lambda y, z: (1 - y, z))
 
 
-def clear_kernel(panel, panel_t):
+def clear_kernel(_, panel, panel_t):
     def clear(j, _):
         panel[j] = jnp.zeros((ROWS * T, T), BF)
         return 0
@@ -81,15 +81,16 @@
 PANELS = (pltpu.VMEM((COLS, ROWS * T, T), BF), pltpu.VMEM((ROWS, COLS * T, T), BF))
 
 
-def cleared():
+def cleared(after):
     return pl.pallas_call(
         clear_kernel,
         out_shape=PANELS,
+        in_specs=[VMEM],
         out_specs=(VMEM, VMEM),
         compiler_params=pltpu.CompilerParams(vmem_limit_bytes=4 * MIB),
         cost_estimate=pl.CostEstimate(flops=0, bytes_accessed=12 * MIB, transcendentals=0),
         name="clear",
-    )()
+    )(after)
 
 
 def dense_kernel(places, tiles, _, __, panel, panel_t, held, place_s, sems, place_sem):
@@ -306,24 +307,6 @@
     )(x, high, low)
 
 
-def stage_kernel(x, out, sem):
-    copy = pltpu.make_async_copy(x, out, sem)
-    copy.start()
-    copy.wait()
-
-
-def stage(x):
-    return pl.pallas_call(
-        stage_kernel,
-        out_shape=pltpu.VMEM(x.shape, x.dtype),
-        in_specs=[HBM],
-        out_specs=VMEM,
-        scratch_shapes=[pltpu.SemaphoreType.DMA],
-        compiler_params=pltpu.CompilerParams(vmem_limit_bytes=4 * MIB),
-        name="stage",
-    )(x)
-
-
 def total_kernel(*refs):
     total = refs[0][...].astype(F32)
     for ref in refs[1:-1]:
@@ -386,19 +369,18 @@
 def shards(
     features, adjacency, tile_row, tile_column, tile_count, weight_in, bias_in, weight_out, bias_out
 ):
+    mine = lax.reduce_precision(features, 8, 7)
     high = to_yhi(features)
     low = to_ylo(features)
-    panels = cleared()
-    own_features = stage(features)
-    places = slots(tile_row, tile_column, tile_count)
-    own_features, places = lax.optimization_barrier((own_features, places))
-    row_pair, col_pair = pair(own_features, high, low)
+    panels = cleared(mine)
+    row_pair, col_pair = pair(mine, high, low)
     row_pairs, col_pairs = [row_pair], [col_pair]
     for d in HOPS[1:]:
         col_pairs.append(to_x(col_pair, d))
         row_pairs.append(to_z(row_pair, d))
 
-    places, _ = lax.optimization_barrier((places, (row_pair, col_pair)))
+    indices, _ = lax.optimization_barrier(((tile_row, tile_column, tile_count), (row_pair, col_pair)))
+    places = slots(*indices)
     panel, panel_t = dense(adjacency[0], places, panels)
     col_pairs = col_pairs + [to_core(block) for block in col_pairs]
 
@@ -406,17 +388,25 @@
     from_other = to_core(to_other)
     own = back(panel_t, row_pairs, tuple((h, 0) for h in HOPS), False)
     chip = join(from_other, own)
-    arrived = [to_x(chip[n], HOPS[n]) for n in (1, 2, 3)]
+    arrived = []
+    for n in (1, 2, 3):
+        arrived.append(to_x(chip[n], HOPS[n]))
 
     sent = [forward(panel, col_pairs, tuple((h, flip) for h in HOPS[1:])) for flip in (1, 0)]
-    on, here = ([to_z(block, h) for block, h in zip(part, HOPS[1:])] for part in sent)
-    stay, turn = forward(panel, col_pairs, ((0, 0), (0, 1)), F32)
+    on, here = [], []
+    for h, block in zip(HOPS[1:], sent[0]):
+        on.append(to_z(block, h))
+    for h, block in zip(HOPS[1:], sent[1]):
+        here.append(to_z(block, h))
+    (turn,) = forward(panel, col_pairs, ((0, 1),), F32)
+    (stay,) = forward(panel, col_pairs, ((0, 0),), F32)
 
     col_keep, col_send = fold(chip[0], arrived)
     col_recv = to_ylo(col_send)
-    row_recv = to_yhi(total(turn, *on))
+    onward = total(turn, *on)
+    row_recv = to_yhi(onward)
     return update(
-        own_features,
+        mine,
         (stay, *here, row_recv, col_keep, col_recv),
         weight_in,
         bias_in,

time: 80 us -> 77.8 us (0.972)
  the two profiles are of different devices: /device:TPU:48 before, /device:TPU:0 now
where the time goes in v2:
time: 77.8 us; the launch traced here: 77.6 us
  starting transfers between devices  30.3 us (39%)
  waiting for transfers between devices  25.9 us (33%)
  Pallas kernels  18.9 us (24%)
  other arithmetic  1.65 us (2%)
  between operations  0.87 us (1%)
    ppermute x11, starting transfers between devices, col_perm(): return lax.ppermute(value, 'col', pairs)  20.5 us
    ppermute x13, waiting for transfers between devices, row_perm(): return lax.ppermute(value, 'row', pairs)  13.7 us
    ppermute x11, waiting for transfers between devices, col_perm(): return lax.ppermute(value, 'col', pairs)  12.2 us
    ppermute x13, starting transfers between devices, row_perm(): return lax.ppermute(value, 'row', pairs)  9.85 us
    pallas_call x4, Pallas kernels, forward(): pl.pallas_call(functools.partial(forward_kernel, targets=targets), out_sh...  5.04 us
    pallas_call x2, Pallas kernels, back(): pl.pallas_call(functools.partial(back_kernel, targets=targets), out_shape...  4.66 us
    pallas_call x1, Pallas kernels, cleared(): pl.pallas_call(clear_kernel, out_shape=PANELS, in_specs=[VMEM], out_specs...  4.38 us
    pallas_call x1, Pallas kernels, dense(): pl.pallas_call(dense_kernel, out_shape=PANELS, in_specs=[HBM, HBM, VMEM,...  3.05 us
  transfers between devices with their start and end apart: 24, of which 13 were waited for; matrix products, arithmetic and copies ran while one was open for 2% of the time, Pallas kernels for 20%

profile of v2, /device:TPU:0, one launch (start us, length us, event | category | flops | bytes accessed | tf_op | source)
XLA Modules:
  0.0 77.6 jit_solution(4662749126109348557)
XLA Ops:
  0.0 3.3 %collective-permute-start = (bf16[256,256]{1,0:T(8,128)(2,1)}, bf16[256,256]{1,0:T(8,128)(2,1)S(1)}, u32[]{:S(2)}, u32[]{:S(2)}) collective-permute-start(bf16[256,256]{1,0:T(8,128)(2,1)} %param.9), channel_id=1, source_target_pairs={{0,4},{1,5},{2,6},{3,7},{4,0},{5,1},{6,2},{7,3},{8,12},{9,13},{10,... | collective-permute-start | bytes 393224 | tf_op jit(solution)/shard_map/ppermute | solution.py:45
  4.0 0.9 %reduce_precision.3.x._.refs_0_ = bf16[256,256]{1,0:T(8,128)(2,1)S(1)} reduce-precision(bf16[256,256]{1,0:T(8,128)(2,1)} %param.9), exponent_bits=8, mantissa_bits=7 | non-fusion elementwise | flops 65536 | bytes 262144 | tf_op jit(solution)/shard_map/reduce_precision | solution.py:372
  5.6 4.4 %clear.1 = (bf16[32,2048,128]{2,1,0:T(8,128)(2,1)S(1)}, bf16[16,4096,128]{2,1,0:T(8,128)(2,1)S(1)}) custom-call(bf16[256,256]{1,0:T(8,128)(2,1)S(1)} %reduce_precision.3.x._.refs_0_), custom_call_target="tpu_custom_call" | custom-call | bytes 12582912 | tf_op jit(solution)/shard_map/clear/pallas_call | solution.py:85
  10.3 2.0 %collective-permute-start.16 = (bf16[512,256]{1,0:T(8,128)(2,1)S(1)}, bf16[512,256]{1,0:T(8,128)(2,1)S(1)}, u32[]{:S(2)}, u32[]{:S(2)}) collective-permute-start(bf16[512,256]{1,0:T(8,128)(2,1)S(1)} %get-tuple-element.30.refs_0_), channel_id=1, source_target_pairs={{0,1},{1,2},{2,3},{3,0},{4,5},{5,6},{6,7},{7,4},{8,9},{9,10},{10,1... | collective-permute-start | bytes 786440 | tf_op jit(solution)/shard_map/ppermute | solution.py:45
  12.2 2.2 %collective-permute-start.17 = (bf16[512,256]{1,0:T(8,128)(2,1)S(1)}, bf16[512,256]{1,0:T(8,128)(2,1)S(1)}, u32[]{:S(2)}, u32[]{:S(2)}) collective-permute-start(bf16[512,256]{1,0:T(8,128)(2,1)S(1)} %get-tuple-element.30.refs_0_), channel_id=1, source_target_pairs={{0,3},{1,0},{2,1},{3,2},{4,7},{5,4},{6,5},{7,6},{8,11},{9,8},{10,9... | collective-permute-start | bytes 786440 | tf_op jit(solution)/shard_map/ppermute | solution.py:45
  14.4 1.8 %collective-permute-start.18 = (bf16[512,256]{1,0:T(8,128)(2,1)S(1)}, bf16[512,256]{1,0:T(8,128)(2,1)S(1)}, u32[]{:S(2)}, u32[]{:S(2)}) collective-permute-start(bf16[512,256]{1,0:T(8,128)(2,1)S(1)} %get-tuple-element.30.refs_0_), channel_id=1, source_target_pairs={{0,2},{1,3},{2,0},{3,1},{4,6},{5,7},{6,4},{7,5},{8,10},{9,11},{10,... | collective-permute-start | bytes 786440 | tf_op jit(solution)/shard_map/ppermute | solution.py:45
  16.9 3.1 %dense.1 = (bf16[32,2048,128]{2,1,0:T(8,128)(2,1)S(1)}, bf16[16,4096,128]{2,1,0:T(8,128)(2,1)S(1)}) custom-call(s32[1,512]{1,0:T(1,128)S(1)} %compare_select_fusion.places, bf16[384,128,128]{2,1,0:T(8,128)(2,1)} %bitcast.7, bf16[32,2048,128]{2,1,0:T(8,128)(2,1)S(1)} %get-tuple-element.35._, ...), custom_call_target="tpu_custom_call", output_to_operand_aliasing={{0}: (2, {}), {1}: (3, {})} | custom-call | bytes 47185920 | tf_op jit(solution)/shard_map/dense/pallas_call | solution.py:154
  20.6 4.3 %collective-permute-done.17.refs_2_ = bf16[512,256]{1,0:T(8,128)(2,1)S(1)} collective-permute-done((bf16[512,256]{1,0:T(8,128)(2,1)S(1)}, bf16[512,256]{1,0:T(8,128)(2,1)S(1)}, u32[]{:S(2)}, u32[]{:S(2)}) %collective-permute-start.17) | collective-permute-done | bytes 262176 | tf_op jit(solution)/shard_map/ppermute | solution.py:45
  24.9 1.8 %collective-permute-done.18.refs_3_ = bf16[512,256]{1,0:T(8,128)(2,1)S(1)} collective-permute-done((bf16[512,256]{1,0:T(8,128)(2,1)S(1)}, bf16[512,256]{1,0:T(8,128)(2,1)S(1)}, u32[]{:S(2)}, u32[]{:S(2)}) %collective-permute-start.18) | collective-permute-done | bytes 262176 | tf_op jit(solution)/shard_map/ppermute | solution.py:45
  26.7 2.3 %back.2 = bf16[2048,256]{1,0:T(8,128)(2,1)S(1)} custom-call(bf16[16,4096,128]{2,1,0:T(8,128)(2,1)S(1)} %get-tuple-element.44.panel_t, bf16[512,256]{1,0:T(8,128)(2,1)S(1)} %get-tuple-element.30.refs_0_, bf16[512,256]{1,0:T(8,128)(2,1)S(1)} %collective-permute-done.16.refs_1_, bf16[512,256]{1,0:T(8,128)(2,1)S(1)} %collective-permute-done.17.refs_2_, ...), custom_call_target="tpu_custom_call" | custom-call | flops 2147483648 | bytes 4194304 | tf_op jit(solution)/shard_map/back/pallas_call | solution.py:229
  29.1 1.6 %collective-permute-start.2 = (bf16[512,256]{1,0:T(8,128)(2,1)S(1)}, bf16[512,256]{1,0:T(8,128)(2,1)S(1)}, u32[]{:S(2)}, u32[]{:S(2)}) collective-permute-start(bf16[512,256]{1,0:T(8,128)(2,1)S(1)} %get-tuple-element.31.refs_0_), channel_id=1, source_target_pairs={{0,16},{8,24},{16,32},{24,40},{32,48},{40,56},{48,0},{56,8},{64,80... | collective-permute-start | bytes 786440 | tf_op jit(solution)/shard_map/ppermute | solution.py:36
  30.7 1.7 %collective-permute-start.3 = (bf16[512,256]{1,0:T(8,128)(2,1)S(1)}, bf16[512,256]{1,0:T(8,128)(2,1)S(1)}, u32[]{:S(2)}, u32[]{:S(2)}) collective-permute-start(bf16[512,256]{1,0:T(8,128)(2,1)S(1)} %get-tuple-element.31.refs_0_), channel_id=1, source_target_pairs={{0,48},{8,56},{16,0},{24,8},{32,16},{40,24},{48,32},{56,40},{64,11... | collective-permute-start | bytes 786440 | tf_op jit(solution)/shard_map/ppermute | solution.py:36
  32.4 1.8 %collective-permute-start.4 = (bf16[512,256]{1,0:T(8,128)(2,1)S(1)}, bf16[512,256]{1,0:T(8,128)(2,1)S(1)}, u32[]{:S(2)}, u32[]{:S(2)}) collective-permute-start(bf16[512,256]{1,0:T(8,128)(2,1)S(1)} %get-tuple-element.31.refs_0_), channel_id=1, source_target_pairs={{0,32},{8,40},{16,48},{24,56},{32,0},{40,8},{48,16},{56,24},{64,96... | collective-permute-start | bytes 786440 | tf_op jit(solution)/shard_map/ppermute | solution.py:36
  34.2 4.8 %collective-permute-done.2.refs_1_ = bf16[512,256]{1,0:T(8,128)(2,1)S(1)} collective-permute-done((bf16[512,256]{1,0:T(8,128)(2,1)S(1)}, bf16[512,256]{1,0:T(8,128)(2,1)S(1)}, u32[]{:S(2)}, u32[]{:S(2)}) %collective-permute-start.2) | collective-permute-done | bytes 262176 | tf_op jit(solution)/shard_map/ppermute | solution.py:36
  39.0 4.9 %collective-permute-done.3.refs_2_ = bf16[512,256]{1,0:T(8,128)(2,1)S(1)} collective-permute-done((bf16[512,256]{1,0:T(8,128)(2,1)S(1)}, bf16[512,256]{1,0:T(8,128)(2,1)S(1)}, u32[]{:S(2)}, u32[]{:S(2)}) %collective-permute-start.3) | collective-permute-done | bytes 262176 | tf_op jit(solution)/shard_map/ppermute | solution.py:36
  44.0 1.7 %collective-permute-done.4.refs_3_ = bf16[512,256]{1,0:T(8,128)(2,1)S(1)} collective-permute-done((bf16[512,256]{1,0:T(8,128)(2,1)S(1)}, bf16[512,256]{1,0:T(8,128)(2,1)S(1)}, u32[]{:S(2)}, u32[]{:S(2)}) %collective-permute-start.4) | collective-permute-done | bytes 262176 | tf_op jit(solution)/shard_map/ppermute | solution.py:36
  45.7 1.5 %collective-permute-done.8.refs_7_ = bf16[512,256]{1,0:T(8,128)(2,1)S(1)} collective-permute-done((bf16[512,256]{1,0:T(8,128)(2,1)S(1)}, bf16[512,256]{1,0:T(8,128)(2,1)S(1)}, u32[]{:S(2)}, u32[]{:S(2)}) %collective-permute-start.8) | collective-permute-done | bytes 262176 | tf_op jit(solution)/shard_map/ppermute | solution.py:36
  47.2 1.8 %forward.7 = (bf16[256,256]{1,0:T(8,128)(2,1)S(1)}, bf16[256,256]{1,0:T(8,128)(2,1)S(1)}, bf16[256,256]{1,0:T(8,128)(2,1)S(1)}) custom-call(bf16[32,2048,128]{2,1,0:T(8,128)(2,1)S(1)} %get-tuple-element.37.panel, bf16[512,256]{1,0:T(8,128)(2,1)S(1)} %get-tuple-element.31.refs_0_, bf16[512,256]{1,0:T(8,128)(2,1)S(1)} %collective-permute-done.2.refs_1_, ...), custom_call_target="tpu_custom_call" | custom-call | flops 1610612736 | bytes 1572864 | tf_op jit(solution)/shard_map/forward/pallas_call | solution.py:261
  49.0 1.4 %collective-permute-start.12 = (bf16[256,256]{1,0:T(8,128)(2,1)S(1)}, bf16[256,256]{1,0:T(8,128)(2,1)S(1)}, u32[]{:S(2)}, u32[]{:S(2)}) collective-permute-start(bf16[256,256]{1,0:T(8,128)(2,1)S(1)} %get-tuple-element.41), channel_id=1, source_target_pairs={{0,1},{1,2},{2,3},{3,0},{4,5},{5,6},{6,7},{7,4},{8,9},{9,10},{10,1... | collective-permute-start | bytes 393224 | tf_op jit(solution)/shard_map/ppermute | solution.py:45
  50.4 2.3 %back.3 = (bf16[512,256]{1,0:T(8,128)(2,1)S(1)}, bf16[512,256]{1,0:T(8,128)(2,1)S(1)}, bf16[512,256]{1,0:T(8,128)(2,1)S(1)}, bf16[512,256]{1,0:T(8,128)(2,1)S(1)}) custom-call(bf16[16,4096,128]{2,1,0:T(8,128)(2,1)S(1)} %get-tuple-element.44.panel_t, bf16[512,256]{1,0:T(8,128)(2,1)S(1)} %get-tuple-element.30.refs_0_, ...), custom_call_target="tpu_custom_call" | custom-call | flops 2147483648 | bytes 4194304 | tf_op jit(solution)/shard_map/back/pallas_call | solution.py:229
  53.0 1.2 %collective-permute-start.20 = (bf16[512,256]{1,0:T(8,128)(2,1)S(1)}, bf16[512,256]{1,0:T(8,128)(2,1)S(1)}, u32[]{:S(2)}, u32[]{:S(2)}) collective-permute-start(bf16[512,256]{1,0:T(8,128)(2,1)S(1)} %get-tuple-element.50), channel_id=1, source_target_pairs={{0,16},{8,24},{16,32},{24,40},{32,48},{40,56},{48,0},{56,8},{64,80... | collective-permute-start | bytes 786440 | tf_op jit(solution)/shard_map/ppermute | solution.py:36
  54.2 2.1 %collective-permute-start.21 = (bf16[512,256]{1,0:T(8,128)(2,1)S(1)}, bf16[512,256]{1,0:T(8,128)(2,1)S(1)}, u32[]{:S(2)}, u32[]{:S(2)}) collective-permute-start(bf16[512,256]{1,0:T(8,128)(2,1)S(1)} %get-tuple-element.51), channel_id=1, source_target_pairs={{0,48},{8,56},{16,0},{24,8},{32,16},{40,24},{48,32},{56,40},{64,11... | collective-permute-start | bytes 786440 | tf_op jit(solution)/shard_map/ppermute | solution.py:36
  56.9 2.1 %collective-permute-start.13 = (bf16[256,256]{1,0:T(8,128)(2,1)S(1)}, bf16[256,256]{1,0:T(8,128)(2,1)S(1)}, u32[]{:S(2)}, u32[]{:S(2)}) collective-permute-start(bf16[256,256]{1,0:T(8,128)(2,1)S(1)} %get-tuple-element.42), channel_id=1, source_target_pairs={{0,3},{1,0},{2,1},{3,2},{4,7},{5,4},{6,5},{7,6},{8,11},{9,8},{10,9... | collective-permute-start | bytes 393224 | tf_op jit(solution)/shard_map/ppermute | solution.py:45
  59.9 1.8 %forward.5 = (bf16[256,256]{1,0:T(8,128)(2,1)S(1)}, bf16[256,256]{1,0:T(8,128)(2,1)S(1)}, bf16[256,256]{1,0:T(8,128)(2,1)S(1)}) custom-call(bf16[32,2048,128]{2,1,0:T(8,128)(2,1)S(1)} %get-tuple-element.37.panel, bf16[512,256]{1,0:T(8,128)(2,1)S(1)} %get-tuple-element.31.refs_0_, bf16[512,256]{1,0:T(8,128)(2,1)S(1)} %collective-permute-done.2.refs_1_, ...), custom_call_target="tpu_custom_call" | custom-call | flops 1610612736 | bytes 1572864 | tf_op jit(solution)/shard_map/forward/pallas_call | solution.py:261
  61.7 1.8 %collective-permute-done.13.refs_2_ = bf16[256,256]{1,0:T(8,128)(2,1)S(1)} collective-permute-done((bf16[256,256]{1,0:T(8,128)(2,1)S(1)}, bf16[256,256]{1,0:T(8,128)(2,1)S(1)}, u32[]{:S(2)}, u32[]{:S(2)}) %collective-permute-start.13) | collective-permute-done | bytes 131104 | tf_op jit(solution)/shard_map/ppermute | solution.py:45
  63.5 3.8 %collective-permute-start.10 = (bf16[256,256]{1,0:T(8,128)(2,1)S(1)}, bf16[256,256]{1,0:T(8,128)(2,1)S(1)}, u32[]{:S(2)}, u32[]{:S(2)}) collective-permute-start(bf16[256,256]{1,0:T(8,128)(2,1)S(1)} %get-tuple-element.39), channel_id=1, source_target_pairs={{0,3},{1,0},{2,1},{3,2},{4,7},{5,4},{6,5},{7,6},{8,11},{9,8},{10,9... | collective-permute-start | bytes 393224 | tf_op jit(solution)/shard_map/ppermute | solution.py:45
  67.5 1.9 %collective-permute-start.9 = (bf16[256,256]{1,0:T(8,128)(2,1)S(1)}, bf16[256,256]{1,0:T(8,128)(2,1)S(1)}, u32[]{:S(2)}, u32[]{:S(2)}) collective-permute-start(bf16[256,256]{1,0:T(8,128)(2,1)S(1)} %get-tuple-element.38), channel_id=1, source_target_pairs={{0,1},{1,2},{2,3},{3,0},{4,5},{5,6},{6,7},{7,4},{8,9},{9,10},{10,1... | collective-permute-start | bytes 393224 | tf_op jit(solution)/shard_map/ppermute | solution.py:45
  69.3 1.8 %collective-permute-start.15 = (bf16[256,256]{1,0:T(8,128)(2,1)S(1)}, bf16[256,256]{1,0:T(8,128)(2,1)S(1)}, u32[]{:S(2)}, u32[]{:S(2)}) collective-permute-start(bf16[256,256]{1,0:T(8,128)(2,1)S(1)} %total.1), channel_id=1, source_target_pairs={{0,4},{1,5},{2,6},{3,7},{4,0},{5,1},{6,2},{7,3},{8,12},{9,13},{10,... | collective-permute-start | bytes 393224 | tf_op jit(solution)/shard_map/ppermute | solution.py:45
  71.4 0.7 forward.4.refs_1_
  72.1 1.8 %collective-permute-done.11.refs_4_ = bf16[256,256]{1,0:T(8,128)(2,1)S(1)} collective-permute-done((bf16[256,256]{1,0:T(8,128)(2,1)S(1)}, bf16[256,256]{1,0:T(8,128)(2,1)S(1)}, u32[]{:S(2)}, u32[]{:S(2)}) %collective-permute-start.11) | collective-permute-done | bytes 131104 | tf_op jit(solution)/shard_map/ppermute | solution.py:45
  74.0 1.2 %collective-permute-done.9.refs_2_ = bf16[256,256]{1,0:T(8,128)(2,1)S(1)} collective-permute-done((bf16[256,256]{1,0:T(8,128)(2,1)S(1)}, bf16[256,256]{1,0:T(8,128)(2,1)S(1)}, u32[]{:S(2)}, u32[]{:S(2)}) %collective-permute-start.9) | collective-permute-done | bytes 131104 | tf_op jit(solution)/shard_map/ppermute | solution.py:45
  76.4 1.2 %update.1 = bf16[256,256]{1,0:T(8,128)(2,1)} custom-call(bf16[256,256]{1,0:T(8,128)(2,1)S(1)} %reduce_precision.3.x._.refs_0_, f32[256,256]{1,0:T(8,128)S(1)} %forward.4.refs_1_, bf16[256,256]{1,0:T(8,128)(2,1)S(1)} %collective-permute-done.9.refs_2_, bf16[256,256]{1,0:T(8,128)(2,1)S(1)} %collective-permute-done.10.refs_3_, ...), custom_call_target="tpu_custom_call" | custom-call | tf_op jit(solution)/shard_map/update/pallas_call | solution.py:359
  (40 shorter events, 5.6 us)
Async XLA Ops:
  0.0 10.0 %collective-permute-start = (bf16[256,256]{1,0:T(8,128)(2,1)}, bf16[256,256]{1,0:T(8,128)(2,1)S(1)}, u32[]{:S(2)}, u32[]{:S(2)}) collective-permute-start(bf16[256,256]{1,0:T(8,128)(2,1)} %param.9), channel_id=1, source_target_pairs={{0,4},{1,5},{2,6},{3,7},{4,0},{5,1},{6,2},{7,3},{8,12},{9,13},{10,... | collective-permute-start | bytes 393224 | tf_op jit(solution)/shard_map/ppermute | solution.py:45
  3.3 6.9 %collective-permute-start.1 = (bf16[256,256]{1,0:T(8,128)(2,1)}, bf16[256,256]{1,0:T(8,128)(2,1)S(1)}, u32[]{:S(2)}, u32[]{:S(2)}) collective-permute-start(bf16[256,256]{1,0:T(8,128)(2,1)} %param.9), channel_id=1, source_target_pairs={{0,64},{8,72},{16,80},{24,88},{32,96},{40,104},{48,112},{56,120},{... | collective-permute-start | bytes 393224 | tf_op jit(solution)/shard_map/ppermute | solution.py:36
  10.3 10.4 %collective-permute-start.16 = (bf16[512,256]{1,0:T(8,128)(2,1)S(1)}, bf16[512,256]{1,0:T(8,128)(2,1)S(1)}, u32[]{:S(2)}, u32[]{:S(2)}) collective-permute-start(bf16[512,256]{1,0:T(8,128)(2,1)S(1)} %get-tuple-element.30.refs_0_), channel_id=1, source_target_pairs={{0,1},{1,2},{2,3},{3,0},{4,5},{5,6},{6,7},{7,4},{8,9},{9,10},{10,1... | collective-permute-start | bytes 786440 | tf_op jit(solution)/shard_map/ppermute | solution.py:45
  12.2 12.6 %collective-permute-start.17 = (bf16[512,256]{1,0:T(8,128)(2,1)S(1)}, bf16[512,256]{1,0:T(8,128)(2,1)S(1)}, u32[]{:S(2)}, u32[]{:S(2)}) collective-permute-start(bf16[512,256]{1,0:T(8,128)(2,1)S(1)} %get-tuple-element.30.refs_0_), channel_id=1, source_target_pairs={{0,3},{1,0},{2,1},{3,2},{4,7},{5,4},{6,5},{7,6},{8,11},{9,8},{10,9... | collective-permute-start | bytes 786440 | tf_op jit(solution)/shard_map/ppermute | solution.py:45
  14.4 12.2 %collective-permute-start.18 = (bf16[512,256]{1,0:T(8,128)(2,1)S(1)}, bf16[512,256]{1,0:T(8,128)(2,1)S(1)}, u32[]{:S(2)}, u32[]{:S(2)}) collective-permute-start(bf16[512,256]{1,0:T(8,128)(2,1)S(1)} %get-tuple-element.30.refs_0_), channel_id=1, source_target_pairs={{0,2},{1,3},{2,0},{3,1},{4,6},{5,7},{6,4},{7,5},{8,10},{9,11},{10,... | collective-permute-start | bytes 786440 | tf_op jit(solution)/shard_map/ppermute | solution.py:45
  29.0 23.7 %collective-permute-start.19 = (bf16[2048,256]{1,0:T(8,128)(2,1)S(1)}, bf16[2048,256]{1,0:T(8,128)(2,1)S(1)}, u32[]{:S(2)}, u32[]{:S(2)}) collective-permute-start(bf16[2048,256]{1,0:T(8,128)(2,1)S(1)} %back.2), channel_id=1, source_target_pairs={{0,8},{8,0},{16,24},{24,16},{32,40},{40,32},{48,56},{56,48},{64,72... | collective-permute-start | bytes 3145736 | tf_op jit(solution)/shard_map/ppermute | solution.py:36
  29.1 9.9 %collective-permute-start.2 = (bf16[512,256]{1,0:T(8,128)(2,1)S(1)}, bf16[512,256]{1,0:T(8,128)(2,1)S(1)}, u32[]{:S(2)}, u32[]{:S(2)}) collective-permute-start(bf16[512,256]{1,0:T(8,128)(2,1)S(1)} %get-tuple-element.31.refs_0_), channel_id=1, source_target_pairs={{0,16},{8,24},{16,32},{24,40},{32,48},{40,56},{48,0},{56,8},{64,80... | collective-permute-start | bytes 786440 | tf_op jit(solution)/shard_map/ppermute | solution.py:36
  30.7 13.3 %collective-permute-start.3 = (bf16[512,256]{1,0:T(8,128)(2,1)S(1)}, bf16[512,256]{1,0:T(8,128)(2,1)S(1)}, u32[]{:S(2)}, u32[]{:S(2)}) collective-permute-start(bf16[512,256]{1,0:T(8,128)(2,1)S(1)} %get-tuple-element.31.refs_0_), channel_id=1, source_target_pairs={{0,48},{8,56},{16,0},{24,8},{32,16},{40,24},{48,32},{56,40},{64,11... | collective-permute-start | bytes 786440 | tf_op jit(solution)/shard_map/ppermute | solution.py:36
  32.4 13.2 %collective-permute-start.4 = (bf16[512,256]{1,0:T(8,128)(2,1)S(1)}, bf16[512,256]{1,0:T(8,128)(2,1)S(1)}, u32[]{:S(2)}, u32[]{:S(2)}) collective-permute-start(bf16[512,256]{1,0:T(8,128)(2,1)S(1)} %get-tuple-element.31.refs_0_), channel_id=1, source_target_pairs={{0,32},{8,40},{16,48},{24,56},{32,0},{40,8},{48,16},{56,24},{64,96... | collective-permute-start | bytes 786440 | tf_op jit(solution)/shard_map/ppermute | solution.py:36
  34.2 11.4 %collective-permute-start.5 = (bf16[512,256]{1,0:T(8,128)(2,1)S(1)}, bf16[512,256]{1,0:T(8,128)(2,1)S(1)}, u32[]{:S(2)}, u32[]{:S(2)}) collective-permute-start(bf16[512,256]{1,0:T(8,128)(2,1)S(1)} %get-tuple-element.31.refs_0_), channel_id=1, source_target_pairs={{0,8},{8,0},{16,24},{24,16},{32,40},{40,32},{48,56},{56,48},{64,72... | collective-permute-start | bytes 786440 | tf_op jit(solution)/shard_map/ppermute | solution.py:36
  39.0 6.6 %collective-permute-start.6 = (bf16[512,256]{1,0:T(8,128)(2,1)S(1)}, bf16[512,256]{1,0:T(8,128)(2,1)S(1)}, u32[]{:S(2)}, u32[]{:S(2)}) collective-permute-start(bf16[512,256]{1,0:T(8,128)(2,1)S(1)} %collective-permute-done.2.refs_1_), channel_id=1, source_target_pairs={{0,8},{8,0},{16,24},{24,16},{32,40},{40,32},{48,56},{56,48},{64,72... | collective-permute-start | bytes 786440 | tf_op jit(solution)/shard_map/ppermute | solution.py:36
  44.0 1.7 %collective-permute-start.7 = (bf16[512,256]{1,0:T(8,128)(2,1)S(1)}, bf16[512,256]{1,0:T(8,128)(2,1)S(1)}, u32[]{:S(2)}, u32[]{:S(2)}) collective-permute-start(bf16[512,256]{1,0:T(8,128)(2,1)S(1)} %collective-permute-done.3.refs_2_), channel_id=1, source_target_pairs={{0,8},{8,0},{16,24},{24,16},{32,40},{40,32},{48,56},{56,48},{64,72... | collective-permute-start | bytes 786440 | tf_op jit(solution)/shard_map/ppermute | solution.py:36
  45.6 1.5 %collective-permute-start.8 = (bf16[512,256]{1,0:T(8,128)(2,1)S(1)}, bf16[512,256]{1,0:T(8,128)(2,1)S(1)}, u32[]{:S(2)}, u32[]{:S(2)}) collective-permute-start(bf16[512,256]{1,0:T(8,128)(2,1)S(1)} %collective-permute-done.4.refs_3_), channel_id=1, source_target_pairs={{0,8},{8,0},{16,24},{24,16},{32,40},{40,32},{48,56},{56,48},{64,72... | collective-permute-start | bytes 786440 | tf_op jit(solution)/shard_map/ppermute | solution.py:36
  49.0 10.7 %collective-permute-start.12 = (bf16[256,256]{1,0:T(8,128)(2,1)S(1)}, bf16[256,256]{1,0:T(8,128)(2,1)S(1)}, u32[]{:S(2)}, u32[]{:S(2)}) collective-permute-start(bf16[256,256]{1,0:T(8,128)(2,1)S(1)} %get-tuple-element.41), channel_id=1, source_target_pairs={{0,1},{1,2},{2,3},{3,0},{4,5},{5,6},{6,7},{7,4},{8,9},{9,10},{10,1... | collective-permute-start | bytes 393224 | tf_op jit(solution)/shard_map/ppermute | solution.py:45
  53.0 14.5 %collective-permute-start.20 = (bf16[512,256]{1,0:T(8,128)(2,1)S(1)}, bf16[512,256]{1,0:T(8,128)(2,1)S(1)}, u32[]{:S(2)}, u32[]{:S(2)}) collective-permute-start(bf16[512,256]{1,0:T(8,128)(2,1)S(1)} %get-tuple-element.50), channel_id=1, source_target_pairs={{0,16},{8,24},{16,32},{24,40},{32,48},{40,56},{48,0},{56,8},{64,80... | collective-permute-start | bytes 786440 | tf_op jit(solution)/shard_map/ppermute | solution.py:36
  54.2 15.2 %collective-permute-start.21 = (bf16[512,256]{1,0:T(8,128)(2,1)S(1)}, bf16[512,256]{1,0:T(8,128)(2,1)S(1)}, u32[]{:S(2)}, u32[]{:S(2)}) collective-permute-start(bf16[512,256]{1,0:T(8,128)(2,1)S(1)} %get-tuple-element.51), channel_id=1, source_target_pairs={{0,48},{8,56},{16,0},{24,8},{32,16},{40,24},{48,32},{56,40},{64,11... | collective-permute-start | bytes 786440 | tf_op jit(solution)/shard_map/ppermute | solution.py:36
  56.3 14.9 %collective-permute-start.22 = (bf16[512,256]{1,0:T(8,128)(2,1)S(1)}, bf16[512,256]{1,0:T(8,128)(2,1)S(1)}, u32[]{:S(2)}, u32[]{:S(2)}) collective-permute-start(bf16[512,256]{1,0:T(8,128)(2,1)S(1)} %get-tuple-element.52), channel_id=1, source_target_pairs={{0,32},{8,40},{16,48},{24,56},{32,0},{40,8},{48,16},{56,24},{64,96... | collective-permute-start | bytes 786440 | tf_op jit(solution)/shard_map/ppermute | solution.py:36
  56.9 6.7 %collective-permute-start.13 = (bf16[256,256]{1,0:T(8,128)(2,1)S(1)}, bf16[256,256]{1,0:T(8,128)(2,1)S(1)}, u32[]{:S(2)}, u32[]{:S(2)}) collective-permute-start(bf16[256,256]{1,0:T(8,128)(2,1)S(1)} %get-tuple-element.42), channel_id=1, source_target_pairs={{0,3},{1,0},{2,1},{3,2},{4,7},{5,4},{6,5},{7,6},{8,11},{9,8},{10,9... | collective-permute-start | bytes 393224 | tf_op jit(solution)/shard_map/ppermute | solution.py:45
  59.7 16.7 %copy-start = (bf16[256,1024]{1,0:T(8,128)(2,1)S(1)}, bf16[256,1024]{1,0:T(8,128)(2,1)}, u32[]{:S(2)}) copy-start(bf16[256,1024]{1,0:T(8,128)(2,1)} %refs_8_.1) | copy-start | bytes 1572868
  59.7 16.7 %copy-start.1 = (bf16[1024,256]{1,0:T(8,128)(2,1)S(1)}, bf16[1024,256]{1,0:T(8,128)(2,1)}, u32[]{:S(2)}) copy-start(bf16[1024,256]{1,0:T(8,128)(2,1)} %refs_10_.1) | copy-start | bytes 1572868
  59.7 16.7 %copy-start.2 = (f32[1024]{0:T(1024)S(1)}, f32[1024]{0:T(1024)}, u32[]{:S(2)}) copy-start(f32[1024]{0:T(1024)} %param.15) | copy-start | bytes 12292
  59.7 16.7 %copy-start.3 = (f32[256]{0:T(256)S(1)}, f32[256]{0:T(256)}, u32[]{:S(2)}) copy-start(f32[256]{0:T(256)} %param.17) | copy-start | bytes 3076
  59.7 7.6 %collective-permute-start.14 = (bf16[256,256]{1,0:T(8,128)(2,1)S(1)}, bf16[256,256]{1,0:T(8,128)(2,1)S(1)}, u32[]{:S(2)}, u32[]{:S(2)}) collective-permute-start(bf16[256,256]{1,0:T(8,128)(2,1)S(1)} %get-tuple-element.43), channel_id=1, source_target_pairs={{0,2},{1,3},{2,0},{3,1},{4,6},{5,7},{6,4},{7,5},{8,10},{9,11},{10,... | collective-permute-start | bytes 393224 | tf_op jit(solution)/shard_map/ppermute | solution.py:45
  63.5 8.6 %collective-permute-start.10 = (bf16[256,256]{1,0:T(8,128)(2,1)S(1)}, bf16[256,256]{1,0:T(8,128)(2,1)S(1)}, u32[]{:S(2)}, u32[]{:S(2)}) collective-permute-start(bf16[256,256]{1,0:T(8,128)(2,1)S(1)} %get-tuple-element.39), channel_id=1, source_target_pairs={{0,3},{1,0},{2,1},{3,2},{4,7},{5,4},{6,5},{7,6},{8,11},{9,8},{10,9... | collective-permute-start | bytes 393224 | tf_op jit(solution)/shard_map/ppermute | solution.py:45
  67.4 6.6 %collective-permute-start.11 = (bf16[256,256]{1,0:T(8,128)(2,1)S(1)}, bf16[256,256]{1,0:T(8,128)(2,1)S(1)}, u32[]{:S(2)}, u32[]{:S(2)}) collective-permute-start(bf16[256,256]{1,0:T(8,128)(2,1)S(1)} %get-tuple-element.40), channel_id=1, source_target_pairs={{0,2},{1,3},{2,0},{3,1},{4,6},{5,7},{6,4},{7,5},{8,10},{9,11},{10,... | collective-permute-start | bytes 393224 | tf_op jit(solution)/shard_map/ppermute | solution.py:45
  67.5 7.7 %collective-permute-start.9 = (bf16[256,256]{1,0:T(8,128)(2,1)S(1)}, bf16[256,256]{1,0:T(8,128)(2,1)S(1)}, u32[]{:S(2)}, u32[]{:S(2)}) collective-permute-start(bf16[256,256]{1,0:T(8,128)(2,1)S(1)} %get-tuple-element.38), channel_id=1, source_target_pairs={{0,1},{1,2},{2,3},{3,0},{4,5},{5,6},{6,7},{7,4},{8,9},{9,10},{10,1... | collective-permute-start | bytes 393224 | tf_op jit(solution)/shard_map/ppermute | solution.py:45
  69.3 6.5 %collective-permute-start.15 = (bf16[256,256]{1,0:T(8,128)(2,1)S(1)}, bf16[256,256]{1,0:T(8,128)(2,1)S(1)}, u32[]{:S(2)}, u32[]{:S(2)}) collective-permute-start(bf16[256,256]{1,0:T(8,128)(2,1)S(1)} %total.1), channel_id=1, source_target_pairs={{0,4},{1,5},{2,6},{3,7},{4,0},{5,1},{6,2},{7,3},{8,12},{9,13},{10,... | collective-permute-start | bytes 393224 | tf_op jit(solution)/shard_map/ppermute | solution.py:45
  71.3 5.0 %collective-permute-start.23 = (bf16[256,256]{1,0:T(8,128)(2,1)S(1)}, bf16[256,256]{1,0:T(8,128)(2,1)S(1)}, u32[]{:S(2)}, u32[]{:S(2)}) collective-permute-start(bf16[256,256]{1,0:T(8,128)(2,1)S(1)} %get-tuple-element.54), channel_id=1, source_target_pairs={{0,64},{8,72},{16,80},{24,88},{32,96},{40,104},{48,112},{56,120},{... | collective-permute-start | bytes 393224 | tf_op jit(solution)/shard_map/ppermute | solution.py:36
